TPU v7x, 128 devices: a whole 4x4x4 slice. The times are simulated.
128 devices in a mesh: lat: 16 (over y, z_hi, core), chan: 8 (over z_lo, x).
Axes of the slice: x: 4, y: 4, z: 4 (z_hi: 2, z_lo: 2; z = z_hi * 2 + z_lo), core: 2. Of those that a mesh axis runs over, the one named last changes fastest.
Arguments:
- state: bfloat16 [64, 512, 1024], P('lat', None, 'chan'), may hold values from -15 to 15
- background: bfloat16 [64, 512, 1024], P('lat', None, 'chan'), may hold values from -15.5 to 15.5
- gain: float32 [1024], replicated, may hold values from 0.5 to 2
- w_query: bfloat16 [1024, 1024], P(None, 'chan'), may hold values from -0.2 to 0.2
- w_key: bfloat16 [1024, 1024], P(None, 'chan'), may hold values from -5 to 5
- w_value: bfloat16 [1024, 1024], P(None, 'chan'), may hold values from -0.1875 to 0.1875
- w_out: bfloat16 [1024, 1024], P('chan'), may hold values from -0.75 to 0.75
- decoder: bfloat16 [1024, 69], P('chan'), may hold values from -0.1875 to 0.1875
- interp: bfloat16 [16, 8, 16, 16, 128, 128], P('lat', 'chan'), may hold values from -0.5 to 0.5
- obs_values: bfloat16 [16, 8, 16, 16, 128], P('lat', 'chan'), may hold values from -6 to 6
- tile_index: int32 [16, 8, 16, 16], P('lat', 'chan'), may hold values from 0 to 1103
- block_count: int32 [16, 8, 16], P('lat', 'chan'), may hold values from 1 to 16, as said below
Outputs:
- misfit: float32 [16, 8, 16, 16, 128], P(None, 'chan', 'lat')
- gradient: float32 [64, 512, 1024], P('lat', None, 'chan')
Inputs may be any that keep to these rules, and one draw needn't show every extreme that they name: `tile_index`: A tile index n names variable n // 16 and the run n % 16 of 128 tokens of the target band. Live slots are the first block_count ones; every draw has a target band that receives 16 blocks from every owner and channel group.
All inputs are finite; a program needn't handle non-finite values.
Results may differ from a plain program's by a relative error of at most 0.02.
The roundings to bfloat16 on the way count: a program that leaves them out, or rounds other values in their place, can miss the bound.
Values may be sent and summed in bfloat16 or wider, within the bound.
A program may use at most 128 MiB of HBM per device.

v0:
```python
import jax
import jax.numpy as jnp
from jax import lax
from jax.sharding import PartitionSpec as P

D = 1024
HD = 64
VARS = 69
CELLS = 128
WC = 256
NC = 512


EPSILON = 1e-05
NEGATIVE = -1e30


def with_halo(array, sides, width):
    for axis, dim in sides:
        size, length = (lax.axis_size(axis), array.shape[dim])
        up = [(i, (i + 1) % size) for i in range(size - 1)]
        down = [(j, i) for i, j in up]
        last = lax.slice_in_dim(array, length - width, length, axis=dim)
        initial = lax.slice_in_dim(array, 0, width, axis=dim)
        before = lax.ppermute(last, axis, up)
        after = lax.ppermute(initial, axis, down)
        array = jnp.concatenate([before, array, after], axis=dim)
    return array


def in_blocks(array, dim, length):
    lengths = array.shape
    parts = array.reshape(*lengths[:dim], length, lengths[dim] // length, *lengths[dim + 1 :])
    return jnp.moveaxis(parts, dim, 0)


def sent_and_summed(array, axis, dim):
    length = lax.axis_size(axis)
    parts = lax.all_to_all(in_blocks(array, dim, length), axis, 0, 0, tiled=True)
    return jnp.sum(parts.astype(jnp.float32), axis=0)


def from_everyone(array, axis):
    copies = jnp.broadcast_to(array, (lax.axis_size(axis), *array.shape))
    return lax.all_to_all(copies, axis, split_axis=0, concat_axis=0, tiled=True)


def of_everyone(array, axis):
    everything = from_everyone(array, axis)
    return jnp.sum(everything.astype(jnp.float32), axis=0)


def in_one_piece(arrays, axis, split_dim, concat_dim, along):
    ends, at = ([], 0)
    for a in arrays[:-1]:
        at += a.shape[along]
        ends.append(at)
    both = jnp.concatenate(arrays, axis=along)
    return tuple(
        jnp.split(
            lax.all_to_all(both, axis, split_axis=split_dim, concat_axis=concat_dim, tiled=True),
            ends,
            axis=along,
        )
    )


def taken_together(array, axis):
    everything = from_everyone(array, axis)
    return jnp.sum(everything, axis=0)


def in_one(arrays, axis):
    ends = [0]
    for a in arrays:
        ends.append(ends[-1] + a.size)
    total = taken_together(jnp.concatenate([a.ravel() for a in arrays]), axis)
    return tuple((total[b:e].reshape(a.shape) for a, b, e in zip(arrays, ends, ends[1:])))


def normalize(state_rows):
    average = jnp.mean(state_rows, axis=-1, keepdims=True)
    centred = state_rows - average
    variance = jnp.mean(centred * centred, axis=-1, keepdims=True)
    inverse = lax.rsqrt(variance + EPSILON)
    return (centred * inverse, inverse)


def window_keys(padded, rows_band):
    stacked = jnp.stack(
        [padded[0:rows_band], padded[1 : rows_band + 1], padded[2 : rows_band + 2]], axis=1
    )
    shaped = stacked.reshape(rows_band, 3, NC // WC, WC, stacked.shape[3], stacked.shape[4])
    shaped = jnp.transpose(shaped, (0, 2, 1, 3, 4, 5))
    return shaped.reshape(rows_band, NC // WC, 3 * WC, stacked.shape[3], stacked.shape[4])


def key_mask(valid_rows):
    rows_band = valid_rows.shape[0] - 2
    triple = jnp.stack(
        [valid_rows[0:rows_band], valid_rows[1 : rows_band + 1], valid_rows[2 : rows_band + 2]],
        axis=1,
    )
    spread = jnp.repeat(triple, WC, axis=1)
    return spread[:, None, None, None, :]


def attend_forward(queries, keys_win, values_win, key_valid):
    scores = jnp.einsum(
        "rwihd,rwjhd->rwhij", queries, keys_win, preferred_element_type=jnp.float32
    ) * HD ** (-0.5)
    scores = jnp.where(key_valid, scores, NEGATIVE)
    highest = jnp.max(scores, axis=-1, keepdims=True)
    exponent = jnp.exp(scores - highest)
    attention = exponent / jnp.sum(exponent, axis=-1, keepdims=True)
    attention_low = attention.astype(jnp.bfloat16)
    mixed_heads = jnp.einsum(
        "rwhij,rwjhd->rwihd", attention_low, values_win, preferred_element_type=jnp.float32
    ).astype(jnp.bfloat16)
    return (attention, attention_low, mixed_heads)


def attend_backward(queries, keys_win, values_win, attention, attention_low, grad_mixed):
    grad_probs = jnp.einsum(
        "rwihd,rwjhd->rwhij", grad_mixed, values_win, preferred_element_type=jnp.float32
    )
    row_delta = jnp.sum(attention * grad_probs, axis=-1, keepdims=True)
    grad_scores = (attention * (grad_probs - row_delta) * HD ** (-0.5)).astype(jnp.bfloat16)
    grad_queries = jnp.einsum(
        "rwhij,rwjhd->rwihd", grad_scores, keys_win, preferred_element_type=jnp.float32
    ).astype(jnp.bfloat16)
    grad_keys = jnp.einsum(
        "rwhij,rwihd->rwjhd", grad_scores, queries, preferred_element_type=jnp.float32
    )
    grad_values = jnp.einsum(
        "rwhij,rwihd->rwjhd", attention_low, grad_mixed, preferred_element_type=jnp.float32
    )
    return (grad_queries, grad_keys, grad_values)


def unwindow(windowed, rows_band):
    width_heads = windowed.shape[3] * windowed.shape[4]
    shaped = windowed.reshape(rows_band, NC // WC, 3, WC, width_heads)
    shaped = jnp.transpose(shaped, (0, 2, 1, 3, 4)).reshape(rows_band, 3, NC, width_heads)
    summed = jnp.zeros((rows_band + 2, NC, width_heads), jnp.float32)
    for offset in range(3):
        summed = summed.at[offset : offset + rows_band].add(shaped[:, offset])
    return summed


def contract_last(left_rows, right_rows):
    return lax.dot_general(
        left_rows, right_rows, (((1,), (1,)), ((), ())), preferred_element_type=jnp.float32
    )


def body(
    state,
    background,
    gain,
    w_query,
    w_key,
    w_value,
    w_out,
    decoder,
    interp,
    obs_values,
    tile_index,
    block_count,
):
    rows_band, columns, width_local = state.shape
    tokens = rows_band * columns
    heads_local = width_local // HD
    chan_pos = lax.axis_index("chan")
    lat_pos = lax.axis_index("lat")
    lat_count = lax.axis_size("lat")
    wide_state = lax.all_gather(state, "chan", axis=2, tiled=True)
    hat_rows, inverse = normalize(wide_state.astype(jnp.float32).reshape(tokens, D))
    normed = (hat_rows * gain).astype(jnp.bfloat16)
    queries = jnp.dot(normed, w_query, preferred_element_type=jnp.float32).astype(jnp.bfloat16)
    keys_local = jnp.dot(normed, w_key, preferred_element_type=jnp.float32).astype(jnp.bfloat16)
    values_local = jnp.dot(normed, w_value, preferred_element_type=jnp.float32).astype(jnp.bfloat16)
    key_pair = jnp.stack([keys_local, values_local]).reshape(2, rows_band, columns, width_local)
    padded = with_halo(key_pair, (("lat", 1),), 1)
    global_rows = lat_pos * rows_band + jnp.arange(rows_band + 2, dtype=jnp.int32) - 1
    valid_rows = (global_rows >= 0) & (global_rows < lat_count * rows_band)
    key_valid = key_mask(valid_rows)
    keys_win = window_keys(padded[0].reshape(rows_band + 2, columns, heads_local, HD), rows_band)
    values_win = window_keys(padded[1].reshape(rows_band + 2, columns, heads_local, HD), rows_band)
    query_win = queries.reshape(rows_band, columns // WC, WC, heads_local, HD)
    attention, attention_low, mixed_heads = attend_forward(
        query_win, keys_win, values_win, key_valid
    )
    attn_part = jnp.dot(
        mixed_heads.reshape(tokens, width_local), w_out, preferred_element_type=jnp.float32
    )
    attn_sum = sent_and_summed(
        attn_part.reshape(rows_band, columns, D).astype(jnp.bfloat16), "chan", 2
    )
    updated = (state.astype(jnp.float32) + attn_sum).astype(jnp.bfloat16)
    fields_part = lax.dot_general(
        decoder,
        updated.reshape(tokens, width_local),
        (((0,), (1,)), ((), ())),
        preferred_element_type=jnp.float32,
    )
    fields = of_everyone(fields_part.astype(jnp.bfloat16), "chan").astype(jnp.float32)
    tiles_here = fields.astype(jnp.bfloat16).reshape(VARS * (tokens // CELLS), CELLS)
    slot_ids = jnp.arange(tile_index.shape[-1], dtype=jnp.int32)
    tiles_in = lax.all_to_all(tile_index, "lat", split_axis=2, concat_axis=0, tiled=True)
    sent_tiles = tiles_here[tiles_in]
    picked = lax.all_to_all(sent_tiles, "lat", split_axis=0, concat_axis=2, tiled=True)
    predicted = jnp.einsum(
        "abcsok,abcsk->abcso", interp, picked, preferred_element_type=jnp.float32
    )
    live_slot = slot_ids < block_count[..., None]
    own_misfit = jnp.where(live_slot[..., None], predicted - obs_values.astype(jnp.float32), 0.0)
    own_adjoint = jnp.einsum(
        "abcsok,abcso->abcsk",
        interp,
        own_misfit.astype(jnp.bfloat16),
        preferred_element_type=jnp.float32,
    )
    adjoint, misfit = tuple(
        (
            part.astype(jnp.float32)
            for part in in_one_piece(
                (own_adjoint.astype(jnp.bfloat16), own_misfit.astype(jnp.bfloat16)), "lat", 2, 0, 1
            )
        )
    )
    grad_tiles = (
        jnp.zeros((tiles_here.shape[0], CELLS), jnp.float32)
        .at[tiles_in.reshape(-1)]
        .add(adjoint.reshape(-1, CELLS))
    )
    grad_tiles = of_everyone(grad_tiles.astype(jnp.bfloat16), "chan").astype(jnp.float32)
    grad_field = grad_tiles.reshape(VARS, tokens)
    grad_update = lax.dot_general(
        grad_field,
        decoder.astype(jnp.float32),
        (((0,), (1,)), ((), ())),
        precision=lax.Precision.HIGHEST,
    )
    grad_low = grad_update.astype(jnp.bfloat16).reshape(rows_band, columns, width_local)
    portion = lax.all_gather(grad_low, "chan", axis=2, tiled=True)
    grad_mixed = contract_last(portion.reshape(tokens, portion.shape[2]), w_out)
    grad_mixed = grad_mixed.astype(jnp.bfloat16).reshape(
        rows_band, columns // WC, WC, heads_local, HD
    )
    grad_queries, grad_keys_win, grad_values_win = attend_backward(
        query_win, keys_win, values_win, attention, attention_low, grad_mixed
    )
    grad_pair = jnp.stack(
        [unwindow(grad_keys_win, rows_band), unwindow(grad_values_win, rows_band)]
    )
    rim_rows = jnp.stack([grad_pair[:, 0], grad_pair[:, rows_band + 1]], axis=1)
    arrived = with_halo(rim_rows.astype(jnp.bfloat16), (("lat", 1),), 1).astype(rim_rows.dtype)
    own_rows = grad_pair[:, 1 : rows_band + 1]
    own_rows = own_rows.at[:, 0].add(arrived[:, 0])
    own_rows = own_rows.at[:, rows_band - 1].add(arrived[:, 3])
    grad_keys = own_rows[0].astype(jnp.bfloat16).reshape(tokens, width_local)
    grad_values = own_rows[1].astype(jnp.bfloat16).reshape(tokens, width_local)
    grad_part = contract_last(grad_queries.reshape(tokens, width_local), w_query)
    grad_part = grad_part + contract_last(grad_keys, w_key)
    grad_part = grad_part + contract_last(grad_values, w_value)
    grad_normed = lax.psum_scatter(
        grad_part.astype(jnp.bfloat16), "chan", scatter_dimension=1, tiled=True
    ).astype(jnp.float32)
    gain_local = lax.dynamic_slice_in_dim(gain, chan_pos * width_local, width_local, 0)
    hat_local = lax.dynamic_slice_in_dim(hat_rows, chan_pos * width_local, width_local, 1)
    grad_hat = grad_normed * gain_local
    row_sum, cross_sum = in_one(
        (
            jnp.sum(grad_hat, axis=-1, keepdims=True),
            jnp.sum(grad_hat * hat_local, axis=-1, keepdims=True),
        ),
        "chan",
    )
    grad_norm = (grad_hat - row_sum / D - hat_local * (cross_sum / D)) * inverse
    state_flat = state.astype(jnp.float32).reshape(tokens, width_local)
    gradient = (
        state_flat
        - background.astype(jnp.float32).reshape(tokens, width_local)
        + grad_update
        + grad_norm
    )
    return (misfit, gradient.reshape(rows_band, columns, width_local))


def solution(mesh):
    return jax.shard_map(
        body,
        mesh=mesh,
        in_specs=(
            P("lat", None, "chan"),
            P("lat", None, "chan"),
            P(),
            P(None, "chan"),
            P(None, "chan"),
            P(None, "chan"),
            P("chan", None),
            P("chan", None),
            P("lat", "chan", None, None, None, None),
            P("lat", "chan", None, None, None),
            P("lat", "chan", None, None),
            P("lat", "chan", None),
        ),
        out_specs=(P(None, "chan", "lat", None, None), P("lat", None, "chan")),
        check_vma=False,
    )
```

profile of v0, /device:TPU:1, one launch (start us, length us, event | category | flops | bytes accessed | tf_op | source)
XLA Modules:
  0.0 622.2 jit_solution(2726166261618390722)
XLA Ops:
  8.0 61.4 %all-gather.3.cloned.1.call-done = bf16[4,512,1024]{2,1,0:T(8,128)(2,1)} async-done(((bf16[4,512,128]{2,1,0:T(8,128)(2,1)}), bf16[4,512,1024]{2,1,0:T(8,128)(2,1)}) %all-gather.3.cloned.1.call-update) | async-done | bytes 4194320 | tf_op jit(solution)/shard_map/all_gather | solution.py:177
  69.4 3.0 convert_reduce_fusion.2
  74.3 4.0 fusion.8
  82.1 3.4 convolution_convert_fusion.3
  88.6 8.3 %collective-permute-start = (bf16[2,1,512,128]{2,3,1,0:T(8,128)(2,1)}, bf16[2,1,512,128]{2,3,1,0:T(8,128)(2,1)}, u32[]{:S(2)}, u32[]{:S(2)}) collective-permute-start(bf16[2,1,512,128]{2,3,1,0:T(8,128)(2,1)} %get-tuple-element.120), channel_id=1, source_target_pairs={{0,8},{8,16},{16,24},{24,32},{32,40},{40,48},{48,56},{56,64},{64,7... | collective-permute-start | bytes 786440 | tf_op jit(solution)/shard_map/ppermute | solution.py:25
  96.9 2.1 collective-permute-start.1
  99.0 4.3 convolution_convert_fusion.1
  103.2 3.2 reshape.585
  106.4 3.5 copy.145
  116.2 3.7 maximum_bitcast_fusion.1
  121.3 2.9 reshape.530
  124.2 3.7 maximum_bitcast_fusion
  129.3 3.1 reshape.528
  132.5 10.3 %fusion.81 = (f32[4,2,2,256]{3,2,1,0:T(2,128)S(1)}, f32[4,2,2,256,768]{4,3,2,1,0:T(8,128)}) fusion(pred[4,768]{1,0:T(4,128)(4,1)S(1)} %bitcast.246, bf16[4,2,256,2,64]{2,4,3,1,0:T(8,128)(2,1)S(1)} %copy-done.15, bf16[4,2,768,2,64]{2,4,3,1,0:T(8,128)(2,1)} %reshape.530), kind=kOutput, calls=%fused_computation.131 | convolution fusion | flops 415236864 | bytes 14699520 | tf_op jit(solution)/shard_map/sub | solution.py:114
  142.7 6.7 %fusion.41 = bf16[4,2,256,2,64]{2,4,3,1,0:T(8,128)(2,1)S(1)} fusion(bf16[4,2,768,2,64]{2,4,3,1,0:T(8,128)(2,1)S(1)} %copy-done.4, f32[4,2,2,256,768]{4,3,2,1,0:T(8,128)} %get-tuple-element.134, f32[4,2,2,256]{3,2,1,0:T(2,128)S(1)} %get-tuple-element.133), kind=kOutput, calls=%fused_computation.56 | convolution fusion | flops 409206784 | bytes 14696448 | tf_op jit(solution)/shard_map/rwhij,rwjhd->rwihd/dot_general | solution.py:117
  152.7 52.0 %all_to_all.60 = bf16[8,4,512,128]{3,2,1,0:T(8,128)(2,1)} all-to-all(bf16[8,4,512,128]{3,2,1,0:T(8,128)(2,1)S(1)} %bitcast.221), channel_id=1, replica_groups=mesh['lat'=16,'chan'=8] {'chan'}, dimensions={0} | all-to-all | bytes 8388608 | tf_op jit(solution)/shard_map/all_to_all | solution.py:39
  204.7 8.4 %all-to-all-start.2 = ((s32[1,1,16,16]{3,1,0,2:T(1,128)}), s32[1,1,16,16]{3,1,0,2:T(1,128)S(1)}, u32[]{:S(2)}, u32[]{:S(2)}) async-start(s32[1,1,16,16]{3,1,0,2:T(1,128)} %bitcast.15), calls=%async_computation.2 | async-start | bytes 16384 | tf_op jit(solution)/shard_map/all_to_all | solution.py:210
  213.2 2.9 convert_reduce_fusion
  217.7 2.4 all-to-all-done.2
  221.8 3.7 all-to-all-start.1
  225.7 29.8 %all-to-all-done.1 = bf16[8,69,2048]{2,1,0:T(8,128)(2,1)S(1)} async-done(((bf16[8,69,2048]{2,1,0:T(8,128)(2,1)}), bf16[8,69,2048]{2,1,0:T(8,128)(2,1)S(1)}, u32[]{:S(2)}, u32[]{:S(2)}) %all-to-all-start.1) | async-done | bytes 2261024 | tf_op jit(solution)/shard_map/all_to_all | solution.py:45
  257.5 5.7 all-to-all-start.3
  264.4 6.0 all-to-all-done.3
  270.4 7.8 %fusion.6 = f32[16,16,1,128]{3,2,1,0:T(1,128)S(1)} fusion(bf16[1,1,16,16,128,128]{5,4,3,2,1,0:T(8,128)(2,1)} %param.36, bf16[16,16,128,1]{2,1,0,3:T(8,128)(2,1)S(1)} %bitcast.237), kind=kOutput, calls=%fused_computation.12 | convolution fusion | flops 8388608 | bytes 8585216 | tf_op jit(solution)/shard_map/abcsok,abcsk->abcso/dot_general | solution.py:213
  278.4 5.7 fusion.4
  284.7 3.7 all-to-all-start.4
  288.5 7.7 %all-to-all-done.4 = bf16[1,2,16,16,128]{4,3,1,0,2:T(8,128)(2,1)S(1)} async-done(((bf16[1,2,16,16,128]{4,3,1,0,2:T(8,128)(2,1)}), bf16[1,2,16,16,128]{4,3,1,0,2:T(8,128)(2,1)S(1)}, u32[]{:S(2)}, u32[]{:S(2)}) %all-to-all-start.4) | async-done | bytes 131104 | tf_op jit(solution)/shard_map/all_to_all | solution.py:61
  298.7 36.9 %all_to_all.61 = bf16[8,1104,128]{2,1,0:T(8,128)(2,1)S(1)} all-to-all(bf16[8,1104,128]{2,1,0:T(8,128)(2,1)S(1)} %broadcast_in_dim.61), channel_id=1, replica_groups=mesh['lat'=16,'chan'=8] {'chan'}, dimensions={0} | all-to-all | bytes 4521984 | tf_op jit(solution)/shard_map/all_to_all | solution.py:45
  336.1 2.2 fusion.82
  338.3 53.3 %all-gather.5.cloned.1.call-done = bf16[4,512,1024]{2,1,0:T(8,128)(2,1)} async-done(((bf16[4,512,128]{2,1,0:T(8,128)(2,1)}), bf16[4,512,1024]{2,1,0:T(8,128)(2,1)}) %all-gather.5.cloned.1.call-update) | async-done | bytes 4194320 | tf_op jit(solution)/shard_map/all_gather | solution.py:246
  391.7 3.4 convolution_convert_fusion
  397.5 6.5 %fusion.30 = f32[4,2,768,2,64]{2,4,3,1,0:T(8,128)S(1)} fusion(bf16[4,2,256,2,64]{2,4,3,1,0:T(8,128)(2,1)} %copy.154, f32[4,2,2,256,768]{4,3,2,1,0:T(8,128)} %get-tuple-element.134, f32[4,2,2,256]{3,2,1,0:T(2,128)S(1)} %get-tuple-element.133), kind=kOutput, calls=%fused_computation.48 | convolution fusion | flops 408944640 | bytes 16269312 | tf_op jit(solution)/shard_map/rwhij,rwihd->rwjhd/dot_general | solution.py:135
  404.0 6.3 %fusion.83 = f32[4,2,2,256,768]{4,3,2,1,0:T(8,128)} fusion(bf16[4,2,256,2,64]{2,4,3,1,0:T(8,128)(2,1)S(1)} %copy-done.10, bf16[4,2,768,2,64]{2,4,3,1,0:T(8,128)(2,1)S(1)} %copy-done.5), kind=kOutput, calls=%fused_computation.133 | convolution fusion | flops 402653184 | bytes 14680064 | tf_op jit(solution)/shard_map/rwihd,rwjhd->rwhij/dot_general | solution.py:124
  410.4 33.2 %fusion.44 = bf16[4,2,256,2,64]{2,4,3,1,0:T(8,128)(2,1)} fusion(bf16[4,2,768,2,64]{2,4,3,1,0:T(8,128)(2,1)} %reshape.530, f32[4,2,2,256,768]{4,3,2,1,0:T(8,128)} %fusion.83, f32[4,2,2,256,768]{4,3,2,1,0:T(8,128)} %get-tuple-element.134, f32[4,2,2,256]{3,2,1,0:T(2,128)S(1)} %get-tuple-element.133), kind=kOutput, calls=%fused_computation.57 | convolution fusion | flops 424940288 | bytes 27279360 | tf_op jit(solution)/shard_map/rwhij,rwjhd->rwihd/dot_general | solution.py:129
  443.6 40.1 %fusion.27 = f32[4,2,768,2,64]{2,4,3,1,0:T(8,128)} fusion(bf16[4,2,256,2,64]{2,4,3,1,0:T(8,128)(2,1)} %copy.145, f32[4,2,2,256,768]{4,3,2,1,0:T(8,128)} %fusion.83, f32[4,2,2,256,768]{4,3,2,1,0:T(8,128)} %get-tuple-element.134, f32[4,2,2,256]{3,2,1,0:T(2,128)S(1)} %get-tuple-element.133), kind=kOutput, calls=%fused_computation.47 | convolution fusion | flops 424678144 | bytes 28852224 | tf_op jit(solution)/shard_map/rwhij,rwihd->rwjhd/dot_general | solution.py:132
  483.7 5.9 reshape.545
  489.6 4.9 copy.177
  494.5 4.9 copy.157
  499.4 3.3 reshape.549
  502.6 3.6 copy.179
  511.0 2.2 reshape.544
  518.3 8.3 %collective-permute-start.2 = (bf16[2,1,512,128]{3,2,1,0:T(8,128)(2,1)S(1)}, bf16[2,1,512,128]{3,2,1,0:T(8,128)(2,1)S(1)}, u32[]{:S(2)}, u32[]{:S(2)}) collective-permute-start(bf16[2,1,512,128]{3,2,1,0:T(8,128)(2,1)S(1)} %get-tuple-element.110), channel_id=1, source_target_pairs={{0,8},{8,16},{16,24},{24,32},{32,40},{40,48},{48,56},{56,64},{64,7... | collective-permute-start | bytes 786440 | tf_op jit(solution)/shard_map/ppermute | solution.py:25
  530.0 5.8 collective-permute-done.3
  538.1 3.2 add_convert_fusion
  541.4 6.5 %copy.182 = bf16[2048,1024]{0,1:T(8,128)(2,1)} copy(bf16[2048,1024]{1,0:T(8,128)(2,1)} %add_convert_fusion) | data formatting | bytes 8388608
  548.9 52.5 %reduce-scatter.4.cloned.1.call-done = bf16[128,2048]{1,0:T(8,128)(2,1)} async-done(((bf16[1024,2048]{1,0:T(8,128)(2,1)}), bf16[128,2048]{1,0:T(8,128)(2,1)}) %reduce-scatter.4.cloned.1.call-update) | async-done | bytes 524304
  604.6 7.8 %all_to_all.62 = f32[8,1,4096]{2,1,0:T(1,128)S(1)} all-to-all(f32[8,1,4096]{2,1,0:T(1,128)S(1)} %broadcast_in_dim.62), channel_id=1, replica_groups=mesh['lat'=16,'chan'=8] {'chan'}, dimensions={0} | all-to-all | bytes 262144 | tf_op jit(solution)/shard_map/all_to_all | solution.py:45
  612.6 2.9 fusion.58
  (145 shorter events, 54.5 us)
Async XLA Ops:
  7.2 143.1 %copy-start = (bf16[128,1024]{1,0:T(8,128)(2,1)S(1)}, bf16[128,1024]{1,0:T(8,128)(2,1)}, u32[]{:S(2)}) copy-start(bf16[128,1024]{1,0:T(8,128)(2,1)} %param.34) | copy-start | bytes 786436
  7.2 62.2 %all-gather.3.cloned.1.call-start = ((), (), s32[]{:S(2)}) async-start(), calls=%async_computation.8 | async-start | bytes 4718592 | tf_op jit(solution)/shard_map/all_gather | solution.py:177
  8.0 66.3 %copy-start.26 = (f32[1024]{0:T(1024)S(1)}, f32[1024]{0:T(1024)}, u32[]{:S(2)}) copy-start(f32[1024]{0:T(1024)} %param.30) | copy-start | bytes 12292
  69.4 3.4 copy-start.2
  74.3 4.0 copy-start.22
  74.3 5.9 copy-start.19
  78.3 2.0 copy-start.8
  80.2 1.9 copy-start.17
  85.6 0.9 copy-start.12
  88.6 25.0 %collective-permute-start = (bf16[2,1,512,128]{2,3,1,0:T(8,128)(2,1)}, bf16[2,1,512,128]{2,3,1,0:T(8,128)(2,1)}, u32[]{:S(2)}, u32[]{:S(2)}) collective-permute-start(bf16[2,1,512,128]{2,3,1,0:T(8,128)(2,1)} %get-tuple-element.120), channel_id=1, source_target_pairs={{0,8},{8,16},{16,24},{24,32},{32,40},{40,48},{48,56},{56,64},{64,7... | collective-permute-start | bytes 786440 | tf_op jit(solution)/shard_map/ppermute | solution.py:25
  96.9 16.7 %collective-permute-start.1 = (bf16[2,1,512,128]{2,3,1,0:T(8,128)(2,1)}, bf16[2,1,512,128]{2,3,1,0:T(8,128)(2,1)}, u32[]{:S(2)}, u32[]{:S(2)}) collective-permute-start(bf16[2,1,512,128]{2,3,1,0:T(8,128)(2,1)} %get-tuple-element.121), channel_id=1, source_target_pairs={{8,0},{16,8},{24,16},{32,24},{40,32},{48,40},{56,48},{64,56},{72,6... | collective-permute-start | bytes 786440 | tf_op jit(solution)/shard_map/ppermute | solution.py:26
  120.0 4.3 copy-start.13
  127.9 4.5 copy-start.15
  132.5 10.3 %copy-start.4 = (bf16[4,2,768,2,64]{2,4,3,1,0:T(8,128)(2,1)S(1)}, bf16[4,2,768,2,64]{2,4,3,1,0:T(8,128)(2,1)}, u32[]{:S(2)}) copy-start(bf16[4,2,768,2,64]{2,4,3,1,0:T(8,128)(2,1)} %reshape.528) | copy-start | bytes 4718596
  204.7 11.3 %copy-start.11 = (bf16[4,512,128]{2,1,0:T(8,128)(2,1)S(1)}, bf16[4,512,128]{2,1,0:T(8,128)(2,1)}, u32[]{:S(2)}) copy-start(bf16[4,512,128]{2,1,0:T(8,128)(2,1)} %param.28) | copy-start | bytes 1572868
  204.7 11.4 %copy-start.14 = (bf16[4,512,128]{2,1,0:T(8,128)(2,1)S(1)}, bf16[4,512,128]{2,1,0:T(8,128)(2,1)}, u32[]{:S(2)}) copy-start(bf16[4,512,128]{2,1,0:T(8,128)(2,1)} %param.29) | copy-start | bytes 1572868
  204.7 15.4 %all-to-all-start.2 = ((s32[1,1,16,16]{3,1,0,2:T(1,128)}), s32[1,1,16,16]{3,1,0,2:T(1,128)S(1)}, u32[]{:S(2)}, u32[]{:S(2)}) async-start(s32[1,1,16,16]{3,1,0,2:T(1,128)} %bitcast.15), calls=%async_computation.2 | async-start | bytes 16384 | tf_op jit(solution)/shard_map/all_to_all | solution.py:210
  213.2 4.1 copy-start.24
  221.8 41.4 %copy-start.27 = (s32[1,1,16]{2,1,0:T(1,128)S(1)}, s32[1,1,16]{2,1,0:T(1,128)}, u32[]{:S(2)}) copy-start(s32[1,1,16]{2,1,0:T(1,128)} %param.39) | copy-start | bytes 196
  221.8 33.6 %all-to-all-start.1 = ((bf16[8,69,2048]{2,1,0:T(8,128)(2,1)}), bf16[8,69,2048]{2,1,0:T(8,128)(2,1)S(1)}, u32[]{:S(2)}, u32[]{:S(2)}) async-start(bf16[8,69,2048]{2,1,0:T(8,128)(2,1)} %broadcast_in_dim.58), calls=%async_computation.1 | async-start | bytes 4718592 | tf_op jit(solution)/shard_map/all_to_all | solution.py:45
  257.5 13.0 %all-to-all-start.3 = ((bf16[16,1,1,16,128]{4,3,2,1,0:T(8,128)(2,1)}), bf16[16,1,1,16,128]{4,3,2,1,0:T(8,128)(2,1)S(1)}, u32[]{:S(2)}, u32[]{:S(2)}) async-start(bf16[16,1,1,16,128]{4,3,2,1,0:T(8,128)(2,1)} %bitcast.18), calls=%async_computation.3 | async-start | bytes 131072 | tf_op jit(solution)/shard_map/all_to_all | solution.py:212
  270.4 7.8 %copy-start.25 = (bf16[1,1,16,16,128]{4,3,2,1,0:T(8,128)(2,1)S(1)}, bf16[1,1,16,16,128]{4,3,2,1,0:T(8,128)(2,1)}, u32[]{:S(2)}) copy-start(bf16[1,1,16,16,128]{4,3,2,1,0:T(8,128)(2,1)} %param.37) | copy-start | bytes 196612
  284.7 11.4 %all-to-all-start.4 = ((bf16[1,2,16,16,128]{4,3,1,0,2:T(8,128)(2,1)}), bf16[1,2,16,16,128]{4,3,1,0,2:T(8,128)(2,1)S(1)}, u32[]{:S(2)}, u32[]{:S(2)}) async-start(bf16[1,2,16,16,128]{4,3,1,0,2:T(8,128)(2,1)} %pad_maximum_fusion.12), calls=%async_computation.4 | async-start | bytes 262144 | tf_op jit(solution)/shard_map/all_to_all | solution.py:61
  288.4 103.2 %all-gather.5.cloned.1.call-start = ((), (), s32[]{:S(2)}) async-start(), calls=%async_computation.9 | async-start | bytes 4718592 | tf_op jit(solution)/shard_map/all_gather | solution.py:246
  338.3 263.1 %reduce-scatter.4.cloned.1.call-start = ((), (), s32[]{:S(2)}) async-start(), calls=%async_computation.10 | async-start | bytes 4718592
  397.5 6.5 %copy-start.5 = (bf16[4,2,768,2,64]{2,4,3,1,0:T(8,128)(2,1)S(1)}, bf16[4,2,768,2,64]{2,4,3,1,0:T(8,128)(2,1)}, u32[]{:S(2)}) copy-start(bf16[4,2,768,2,64]{2,4,3,1,0:T(8,128)(2,1)} %reshape.528) | copy-start | bytes 4718596
  397.5 6.6 %copy-start.10 = (bf16[4,2,256,2,64]{2,4,3,1,0:T(8,128)(2,1)S(1)}, bf16[4,2,256,2,64]{2,4,3,1,0:T(8,128)(2,1)}, u32[]{:S(2)}) copy-start(bf16[4,2,256,2,64]{2,4,3,1,0:T(8,128)(2,1)} %copy.154) | copy-start | bytes 1572868
  506.2 1.6 copy-start.3
  508.0 1.7 copy-start.16
  518.0 10.6 %copy-start.9 = (bf16[2048,128]{0,1:T(8,128)(2,1)S(1)}, bf16[2048,128]{0,1:T(8,128)(2,1)}, u32[]{:S(2)}) copy-start(bf16[2048,128]{0,1:T(8,128)(2,1)} %reshape.544) | copy-start | bytes 1572868
  518.0 10.6 %copy-start.21 = (bf16[1024,128]{1,0:T(8,128)(2,1)S(1)}, bf16[1024,128]{1,0:T(8,128)(2,1)}, u32[]{:S(2)}) copy-start(bf16[1024,128]{1,0:T(8,128)(2,1)} %param.31) | copy-start | bytes 786436
  518.3 11.7 %collective-permute-start.2 = (bf16[2,1,512,128]{3,2,1,0:T(8,128)(2,1)S(1)}, bf16[2,1,512,128]{3,2,1,0:T(8,128)(2,1)S(1)}, u32[]{:S(2)}, u32[]{:S(2)}) collective-permute-start(bf16[2,1,512,128]{3,2,1,0:T(8,128)(2,1)S(1)} %get-tuple-element.110), channel_id=1, source_target_pairs={{0,8},{8,16},{16,24},{24,32},{32,40},{40,48},{48,56},{56,64},{64,7... | collective-permute-start | bytes 786440 | tf_op jit(solution)/shard_map/ppermute | solution.py:25
  526.6 9.2 %collective-permute-start.3 = (bf16[2,1,512,128]{3,2,1,0:T(8,128)(2,1)S(1)}, bf16[2,1,512,128]{3,2,1,0:T(8,128)(2,1)S(1)}, u32[]{:S(2)}, u32[]{:S(2)}) collective-permute-start(bf16[2,1,512,128]{3,2,1,0:T(8,128)(2,1)S(1)} %get-tuple-element.111), channel_id=1, source_target_pairs={{8,0},{16,8},{24,16},{32,24},{40,32},{48,40},{56,48},{64,56},{72,6... | collective-permute-start | bytes 786440 | tf_op jit(solution)/shard_map/ppermute | solution.py:26
  535.9 1.0 copy-start.18
  536.8 1.3 copy-start.20
  547.9 64.7 %copy-start.6 = (f32[4,512,128]{2,1,0:T(8,128)S(1)}, f32[4,512,128]{2,1,0:T(8,128)}, u32[]{:S(2)}) copy-start(f32[4,512,128]{2,1,0:T(8,128)} %get-tuple-element.122) | copy-start | bytes 3145732
  547.9 64.7 %copy-start.7 = (f32[2048,128]{1,0:T(8,128)S(1)}, f32[2048,128]{1,0:T(8,128)}, u32[]{:S(2)}) copy-start(f32[2048,128]{1,0:T(8,128)} %get-tuple-element.136) | copy-start | bytes 3145732
  547.9 64.7 %copy-start.23 = (f32[1,4,4,128]{3,1,2,0:T(4,128)S(1)}, f32[1,4,4,128]{3,1,2,0:T(4,128)}, u32[]{:S(2)}) copy-start(f32[1,4,4,128]{3,1,2,0:T(4,128)} %copy-done.22) | copy-start | bytes 24580
  547.9 67.5 %copy-start.1 = (bf16[128,1024]{1,0:T(8,128)(2,1)S(1)}, bf16[128,1024]{1,0:T(8,128)(2,1)}, u32[]{:S(2)}) copy-start(bf16[128,1024]{1,0:T(8,128)(2,1)} %param.34) | copy-start | bytes 786436
Sparse Core Ops, SparseCore 0:
  9.6 59.8 all-gather.2
  338.4 53.1 all-gather.4
  548.0 53.2 reduce-scatter.3
where the time goes:
time: 629 us; the launch traced here: 622 us
  waiting for transfers between devices  220 us (35%)
  matrix products  139 us (22%)
  blocking collectives  96.8 us (15%)
  local copies, waits for them, and re-layouts  73.5 us (12%)
  starting transfers between devices  42.3 us (7%)
  other arithmetic  36.7 us (6%)
  between operations  14.7 us (2%)
    all_gather x1, waiting for transfers between devices, body(): wide_state = lax.all_gather(state, 'chan', axis=2, tiled=True)  61.4 us
    all_gather x1, waiting for transfers between devices, body(): portion = lax.all_gather(grad_low, 'chan', axis=2, tiled=True)  53.3 us
    unnamed x4, waiting for transfers between devices  53.2 us
    all_to_all x1, blocking collectives, sent_and_summed(): lax.all_to_all(in_blocks(array, dim, length), axis, 0, 0, tiled=True)  52 us
    all_to_all x2, blocking collectives, from_everyone(): return lax.all_to_all(copies, axis, split_axis=0, concat_axis=0, tiled=True)  44.8 us
    dot_general x1, matrix products, attend_backward(): jnp.einsum('rwhij,rwihd->rwjhd', grad_scores, queries, preferred_element_...  40.1 us
    dot_general x1, matrix products, attend_backward(): jnp.einsum('rwhij,rwjhd->rwihd', grad_scores, keys_win, preferred_element...  33.2 us
    all_to_all x1, waiting for transfers between devices, from_everyone(): return lax.all_to_all(copies, axis, split_axis=0, concat_axis=0, tiled=True)  29.8 us
  transfers between devices with their start and end apart: 11, of which 8 were waited for; matrix products, arithmetic and copies ran while one was open for 4% of the time, Pallas kernels for 0%

commit v1 on v0

v1 whole, which is shorter than its diff:
```python
import functools

import jax
import jax.numpy as jnp
from jax import lax
from jax.experimental import pallas as pl
from jax.experimental.pallas import tpu as pltpu
from jax.sharding import PartitionSpec as P

D = 1024
HD = 64
VARS = 69
EPSILON = 1e-05
VP = 80
T = 256
G = 8
L = 16
BIG = 1e30
MESH = pl.DeviceIdType.MESH
BF = jnp.bfloat16
F32 = jnp.float32
VMEM_LIMIT = 62 * 1024 * 1024


def nn(a, b):
    return lax.dot_general(a, b, (((1,), (0,)), ((), ())), preferred_element_type=F32)


def nt(a, b):
    return lax.dot_general(a, b, (((1,), (1,)), ((), ())), preferred_element_type=F32)


def place():
    b = lax.axis_index("lat")
    c = lax.axis_index("chan")
    k = b % 2
    x = c % 4
    r = x + k * (3 - 2 * x)
    return b, c, r, c // 4, k


def row_of(c, k):
    x = c % 4
    return x + k * (3 - 2 * x)


def neighbours():
    b, c, r, w, k = place()
    inner_up = (r > 0).astype(jnp.int32)
    inner_down = (r < 3).astype(jnp.int32)
    up = (b - 1 + inner_up, c + inner_up * (2 * k - 1))
    down = (b + 1 - inner_down, c + inner_down * (1 - 2 * k))
    row = b * 4 + r
    return up, down, row > 0, row < 4 * L - 1


def chan_peer(i):
    b, c, _, _, _ = place()
    return (b, (c + i) % G)


def lat_peer(i):
    b, c, _, _, _ = place()
    return ((b + i) % L, c)


def greet(chan=True, lat=False, rows=False):
    barrier = pltpu.get_barrier_semaphore()
    count = 0
    if chan:
        for i in range(1, G):
            pl.semaphore_signal(barrier, inc=1, device_id=chan_peer(i), device_id_type=MESH)
            count += 1
    if lat:
        for i in range(1, L):
            pl.semaphore_signal(barrier, inc=1, device_id=lat_peer(i), device_id_type=MESH)
            count += 1
    pl.semaphore_wait(barrier, count)


def remote(src, dst, ss, rs, dev):
    return pltpu.make_async_remote_copy(
        src_ref=src, dst_ref=dst, send_sem=ss, recv_sem=rs, device_id=dev, device_id_type=MESH
    )


def call(kernel, out_shape, in_specs, out_specs, scratch, cid, name, args):
    return pl.pallas_call(
        kernel,
        out_shape=out_shape,
        in_specs=in_specs,
        out_specs=out_specs,
        scratch_shapes=scratch,
        compiler_params=pltpu.CompilerParams(
            collective_id=cid, has_side_effects=cid is not None, vmem_limit_bytes=VMEM_LIMIT
        ),
        name=name,
    )(*args)


VM = pl.BlockSpec(memory_space=pltpu.VMEM)
ANY = pl.BlockSpec(memory_space=pl.ANY)
DMA = pltpu.SemaphoreType.DMA


def sds(shape, dtype):
    return jax.ShapeDtypeStruct(shape, dtype)


def gather_kernel(
    state, w3, wo, dec, idx, zero, x_out, w_out, o_out, d_out, i_out,
    s_state, r_state, s_w, r_w, s_o, r_o, s_d, r_d, s_i, r_i, s_h, r_h, f_w, g_w, f_o, g_o, loc,
):
    b, c, r, w, k = place()
    up, down, has_up, has_down = neighbours()
    greet(chan=True, lat=True)
    partner = (b + 1 - 2 * k, c)

    local = [
        pltpu.make_async_copy(state.at[r, pl.ds(w * T, T)], x_out.at[1, c], loc.at[0]),
        pltpu.make_async_copy(w3, w_out.at[c], loc.at[1]),
        pltpu.make_async_copy(wo, o_out.at[c], loc.at[2]),
        pltpu.make_async_copy(dec, d_out.at[c], loc.at[3]),
        pltpu.make_async_copy(idx.at[b], i_out.at[b], loc.at[4]),
    ]
    for copy in local:
        copy.start()

    @pl.when(jnp.logical_not(has_up))
    def _():
        copy = pltpu.make_async_copy(zero, x_out.at[0], loc.at[5])
        copy.start()
        copy.wait()

    @pl.when(jnp.logical_not(has_down))
    def _():
        copy = pltpu.make_async_copy(zero, x_out.at[2], loc.at[5])
        copy.start()
        copy.wait()

    send = []
    states, weights, outs = {}, {}, {}
    for i in range(1, G):
        _, pc = chan_peer(i)
        pr = row_of(pc, k)
        copy = remote(state.at[pr, pl.ds((pc // 4) * T, T)], x_out.at[1, c], s_state.at[i], r_state.at[i], (b, pc))
        copy.start()
        states[i] = copy
    half = pl.ds(k * 512, 512)
    ohalf = pl.ds(k * 64, 64)
    for i in range(1, G):
        copy = remote(w3.at[half], w_out.at[c, half], s_w.at[i], r_w.at[i], chan_peer(i))
        copy.start()
        weights[i] = copy
    for i in range(1, L):
        dev = lat_peer(i)
        copy = remote(idx.at[dev[0]], i_out.at[b], s_i.at[i], r_i.at[i], dev)
        copy.start()
        send.append(copy)
    for i in range(1, G):
        copy = remote(wo.at[ohalf], o_out.at[c, ohalf], s_o.at[i], r_o.at[i], chan_peer(i))
        copy.start()
        outs[i] = copy
        copy = remote(dec, d_out.at[c], s_d.at[i], r_d.at[i], chan_peer(i))
        copy.start()
        send.append(copy)

    def halo(g, sem, start):
        @pl.when(has_up)
        def _():
            copy = remote(x_out.at[1, g], x_out.at[2, g], s_h.at[0, sem], r_h.at[0, sem], up)
            copy.start() if start else copy.wait_send()

        @pl.when(has_down)
        def _():
            copy = remote(x_out.at[1, g], x_out.at[0, g], s_h.at[1, sem], r_h.at[1, sem], down)
            copy.start() if start else copy.wait_send()

    local[0].wait()
    halo(c, 0, True)
    for i in range(1, G):
        states[i].wait_recv()
        halo((c + G - i) % G, i, True)
    forward = []
    for i in range(1, G):
        g = (c + G - i) % G
        weights[i].wait_recv()
        copy = remote(w_out.at[g, half], w_out.at[g, half], f_w.at[i], g_w.at[i], partner)
        copy.start()
        forward.append(copy)
    for i in range(1, G):
        g = (c + G - i) % G
        outs[i].wait_recv()
        copy = remote(o_out.at[g, ohalf], o_out.at[g, ohalf], f_o.at[i], g_o.at[i], partner)
        copy.start()
        forward.append(copy)
    for copy in forward:
        copy.wait()
    for copy in send:
        copy.wait()
    for i in range(1, G):
        states[i].wait_send()
        weights[i].wait_send()
        outs[i].wait_send()
    for i in range(G):
        halo((c + G - i) % G, i, False)

        @pl.when(has_down)
        def _():
            remote(x_out.at[1, 0], x_out.at[2, 0], s_h.at[0, i], r_h.at[0, i], up).wait_recv()

        @pl.when(has_up)
        def _():
            remote(x_out.at[1, 0], x_out.at[0, 0], s_h.at[1, i], r_h.at[1, i], down).wait_recv()

    for copy in local[1:]:
        copy.wait()


def gather(state, w3, wo, dec, idx):
    zero = jnp.zeros((G, T, 128), BF)
    shapes = (
        sds((3, G, T, 128), BF),
        sds((G, D, 384), BF),
        sds((G, 128, D), BF),
        sds((G, VP, 128), BF),
        sds((L, 16, 128), jnp.int32),
    )
    seven, fifteen = DMA((G,)), DMA((L,))
    scratch = [seven, seven, seven, seven, seven, seven, seven, seven, fifteen, fifteen, DMA((2, G)), DMA((2, G)), seven, seven, seven, seven, DMA((6,))]
    return call(gather_kernel, shapes, [ANY] * 6, [ANY] * 5, scratch, 0, "gather", (state, w3, wo, dec, idx, zero))


def wide(ref, h):
    return jnp.concatenate([ref[h, g] for g in range(G)], axis=1)


def moments(x):
    mean = jnp.sum(x, axis=-1, keepdims=True) * (1.0 / D)
    centred = x - mean
    var = jnp.sum(centred * centred, axis=-1, keepdims=True) * (1.0 / D)
    inv = lax.rsqrt(var + EPSILON)
    return centred * inv, inv


def halves(shape):
    lane = lax.broadcasted_iota(jnp.int32, shape, 1)
    return lane < HD


def only(value, hh):
    first = halves(value.shape)
    keep = first if hh == 0 else jnp.logical_not(first)
    return jnp.where(keep, value, jnp.zeros_like(value))


def row_bias():
    _, _, has_up, has_down = neighbours()
    return (
        jnp.where(has_up, 0.0, -BIG).astype(F32),
        jnp.where(has_down, 0.0, -BIG).astype(F32),
    )


def forward_kernel(x_ref, gain, w_ref, wo_ref, dec_ref, q_ref, kv_ref, t_ref, ml_ref, f_ref, n_ref, acc):
    up_bias, down_bias = row_bias()
    for h in range(3):
        hat, _ = moments(wide(x_ref, h).astype(F32))
        n_ref[pl.ds(h * T, T), :] = (hat * gain[...]).astype(BF)

    def project(g, carry):
        res = nn(n_ref[...], w_ref[g])
        q_ref[g] = res[:, :128].astype(BF)
        kv_ref[0, g] = res[:, 128:256].astype(BF)
        kv_ref[1, g] = res[:, 256:].astype(BF)
        t_ref[0, g] = jnp.transpose(res[:, 128:256]).astype(BF)
        t_ref[1, g] = jnp.transpose(res[:, 256:]).astype(BF)
        return carry

    lax.fori_loop(0, G, project, 0)
    acc[...] = jnp.zeros_like(acc)

    def attend(g, carry):
        query = q_ref[g, pl.ds(T, T), :] * jnp.asarray(0.125, BF)
        parts = []
        for hh in range(2):
            q = only(query, hh)
            s = nt(kv_ref[0, g], q)
            m0 = jnp.max(s[:T], axis=0, keepdims=True) + up_bias
            m1 = jnp.max(s[T : 2 * T], axis=0, keepdims=True)
            m2 = jnp.max(s[2 * T :], axis=0, keepdims=True) + down_bias
            m = jnp.maximum(jnp.maximum(m0, m1), m2)
            e0 = jnp.exp(s[:T] - (m - up_bias))
            e1 = jnp.exp(s[T : 2 * T] - m)
            e2 = jnp.exp(s[2 * T :] - (m - down_bias))
            l = jnp.sum(e0, axis=0, keepdims=True) + jnp.sum(e1, axis=0, keepdims=True) + jnp.sum(e2, axis=0, keepdims=True)
            inv = 1.0 / l
            p = jnp.concatenate([(e0 * inv).astype(BF), (e1 * inv).astype(BF), (e2 * inv).astype(BF)], axis=0)
            parts.append(nn(t_ref[1, g, pl.ds(hh * HD, HD), :], p))
            ml_ref[0, 2 * g + hh] = m
            ml_ref[1, 2 * g + hh] = inv
        mixed = jnp.transpose(jnp.concatenate(parts, axis=0)).astype(BF)
        acc[...] += nn(mixed, wo_ref[g]).astype(BF).astype(F32)
        return carry

    lax.fori_loop(0, G, attend, 0)
    updated = (wide(x_ref, 1).astype(F32) + acc[...]).astype(BF)
    dec = jnp.concatenate([dec_ref[g] for g in range(G)], axis=1)
    f_ref[...] = nt(dec, updated).astype(BF)


def forward(x, gain, w, wo, dec):
    shapes = (
        sds((G, 3 * T, 128), BF),
        sds((2, G, 3 * T, 128), BF),
        sds((2, G, 128, 3 * T), BF),
        sds((2, 16, 1, T), F32),
        sds((VP, T), BF),
    )
    scratch = [pltpu.VMEM((3 * T, D), BF), pltpu.VMEM((T, D), F32)]
    return call(forward_kernel, shapes, [VM] * 5, [VM] * 5, scratch, None, "forward", (x, gain, w, wo, dec))


def swap_rows(src, above, below, ss, rs):
    up, down, has_up, has_down = neighbours()
    to_up = remote(src, below, ss.at[0], rs.at[0], up)
    to_down = remote(src, above, ss.at[1], rs.at[1], down)

    def start():
        pl.when(has_up)(lambda: to_up.start())
        pl.when(has_down)(lambda: to_down.start())

    def wait():
        @pl.when(has_up)
        def _():
            to_up.wait_send()
            to_down.wait_recv()

        @pl.when(has_down)
        def _():
            to_down.wait_send()
            to_up.wait_recv()

    return start, wait


def run_of(c, half, k):
    return row_of(c, k) * 4 + (c // 4) * 2 + half


def pick_kernel(f_ref, ml_ref, idx_ref, mlh_ref, picked, fields, mine, s_f, r_f, s_p, r_p, s_m, r_m):
    b, c, r, w, k = place()
    _, _, has_up, has_down = neighbours()
    mlh_ref[:, 0] = jnp.full((2, 16, 1, T), BIG, F32)
    mlh_ref[:, 1] = jnp.zeros((2, 16, 1, T), F32)
    greet(chan=True, lat=True)
    copies = []
    for i in range(1, G):
        copy = remote(f_ref, fields.at[c, pl.ds(0, VP)], s_f.at[i], r_f.at[i], chan_peer(i))
        copy.start()
        copies.append(copy)
    start, wait = swap_rows(ml_ref, mlh_ref.at[0], mlh_ref.at[1], s_m, r_m)
    start()
    fields[c, pl.ds(0, VP), :] = f_ref[...]
    index = idx_ref[...].reshape(16 * L, 128)
    sixteen = lax.broadcasted_iota(jnp.int32, (16 * L, 128), 1) * 16

    def one(g, total):
        for half in range(2):
            hot = (index == sixteen + run_of(g, half, k)).astype(F32).astype(BF)
            total = total + nn(hot[:, :VP], fields[g, :, pl.ds(half * 128, 128)])
        return total

    total = one(c, jnp.zeros((16 * L, 128), F32))
    for i in range(1, G):
        copies[i - 1].wait_recv()
        total = one((c + G - i) % G, total)
    mine[...] = total.astype(BF).reshape(L, 16, 128)
    sends = []
    for i in range(1, L):
        dev = lat_peer(i)
        copy = remote(mine.at[dev[0]], picked.at[b], s_p.at[i], r_p.at[i], dev)
        copy.start()
        sends.append(copy)
    picked[b] = mine[b]
    for copy in sends:
        copy.wait()
    for copy in copies:
        copy.wait_send()
    wait()


def pick(f, ml, idx):
    shapes = (sds((2, 2, 16, 1, T), F32), sds((L, 16, 128), BF))
    scratch = [pltpu.VMEM((G, VP, T), BF), pltpu.VMEM((L, 16, 128), BF), DMA((G,)), DMA((G,)), DMA((L,)), DMA((L,)), DMA((2,)), DMA((2,))]
    return call(pick_kernel, shapes, [VM] * 3, [VM] * 2, scratch, 1, "pick", (f, ml, idx))


def observe_kernel(count, picked, interp, obs, out, pred, adj):
    b = pl.program_id(0)
    live = count[b]
    pred[...] = jnp.zeros_like(pred)
    adj[...] = jnp.zeros_like(adj)
    row = lax.broadcasted_iota(jnp.int32, (16, 128), 0)

    def predict(s, carry):
        pred[...] = jnp.where(row == s, nt(picked[0], interp[0, s]), pred[...])
        return carry

    lax.fori_loop(0, live, predict, 0)
    misfit = jnp.where(row < live, pred[...] - obs[0].astype(F32), 0.0)
    low = misfit.astype(BF)

    def back(s, carry):
        adj[...] = jnp.where(row == s, nn(low, interp[0, s]), adj[...])
        return carry

    lax.fori_loop(0, live, back, 0)
    out[0, :16, :] = adj[...].astype(BF)
    out[0, 16:, :] = low


def observe(count, picked, interp, obs):
    return pl.pallas_call(
        observe_kernel,
        out_shape=sds((L, 32, 128), BF),
        grid_spec=pltpu.PrefetchScalarGridSpec(
            num_scalar_prefetch=1,
            grid=(L,),
            in_specs=[
                pl.BlockSpec((1, 16, 128), lambda i, n: (i, 0, 0)),
                pl.BlockSpec((1, 16, 128, 128), lambda i, n: (i, 0, 0, 0)),
                pl.BlockSpec((1, 16, 128), lambda i, n: (i, 0, 0)),
            ],
            out_specs=pl.BlockSpec((1, 32, 128), lambda i, n: (i, 0, 0)),
            scratch_shapes=[pltpu.VMEM((16, 128), F32), pltpu.VMEM((16, 128), F32)],
        ),
        name="observe",
    )(count, picked, interp, obs)


def settle_kernel(am, idx_ref, misfit, gf, came, parts, got, s_a, r_a, s_g, r_g, s_h, r_h):
    b, c, r, w, k = place()
    gf[...] = jnp.zeros_like(gf)
    greet(chan=True, lat=True)
    copies = []
    for i in range(1, L):
        dev = lat_peer(i)
        copy = remote(am.at[dev[0]], came.at[b], s_a.at[i], r_a.at[i], dev)
        copy.start()
        copies.append(copy)
    came[b] = am[b]
    index = jnp.transpose(idx_ref[...].reshape(16 * L, 128).astype(F32))
    sixteen = lax.broadcasted_iota(jnp.int32, (VP, 16 * L), 0) * 16
    index = index[:VP].astype(jnp.int32)
    for copy in copies:
        copy.wait()
    all_in = came[...]
    misfit[...] = all_in[:, 16:, :].astype(F32)
    adjoint = all_in[:, :16, :].reshape(16 * L, 128)
    sends = []
    for i in list(range(1, G)) + [0]:
        g = (c + i) % G
        for half in range(2):
            hot = (index == sixteen + run_of(g, half, k)).astype(F32).astype(BF)
            parts[g, :, pl.ds(half * 128, 128)] = nn(hot, adjoint).astype(BF)
        if i:
            copy = remote(parts.at[g], got.at[c], s_g.at[i], r_g.at[i], (b, g))
            copy.start()
            sends.append(copy)
    total = parts[c].astype(F32)
    for i in range(1, G):
        sends[i - 1].wait_recv()
        total = total + got[(c + G - i) % G].astype(F32)
    gf[1] = total
    start, wait = swap_rows(gf.at[1], gf.at[0], gf.at[2], s_h, r_h)
    start()
    for copy in sends:
        copy.wait_send()
    wait()


def settle(am, idx):
    shapes = (sds((L, 16, 128), F32), sds((3, VP, T), F32))
    scratch = [pltpu.VMEM((L, 32, 128), BF), pltpu.VMEM((G, VP, T), BF), pltpu.VMEM((G, VP, T), BF), DMA((L,)), DMA((L,)), DMA((G,)), DMA((G,)), DMA((2,)), DMA((2,))]
    return call(settle_kernel, shapes, [VM] * 2, [VM] * 2, scratch, 2, "settle", (am, idx))


def backward_kernel(
    x_ref, gain, w_ref, wo_ref, dec_ref, q_ref, kv_ref, t_ref, ml_ref, mlh_ref, gf_ref,
    back, gu, low, do, dq, dkv, delta, delta_h, gn, outgo, s_d, r_d, s_y, r_y,
):
    b, c, r, w, k = place()
    up_bias, down_bias = row_bias()
    delta_h[...] = jnp.zeros_like(delta_h)
    greet(chan=True, lat=True)
    dec = jnp.concatenate([dec_ref[g] for g in range(G)], axis=1)
    dec = jnp.concatenate([dec, jnp.zeros((128 - VP, D), BF)], axis=0)
    dec3 = jnp.concatenate([dec, dec, dec], axis=0)
    for h in range(3):
        field = jnp.transpose(jnp.concatenate([gf_ref[h], jnp.zeros((128 - VP, T), F32)], axis=0))
        hi = field.astype(BF)
        rest = field - hi.astype(F32)
        mid = rest.astype(BF)
        lo = (rest - mid.astype(F32)).astype(BF)
        update = nn(jnp.concatenate([hi, mid, lo], axis=1), dec3)
        if h == 1:
            gu[...] = update
        low[pl.ds(h * T, T), :] = update.astype(BF)

    def mixed(g, carry):
        do[g] = nt(low[...], wo_ref[g]).astype(BF)
        return carry

    lax.fori_loop(0, G, mixed, 0)
    mid_rows = pl.ds(T, T)

    def own(g, carry):
        query = q_ref[g, mid_rows, :] * jnp.asarray(0.125, BF)
        parts = []
        dk = jnp.zeros((T, 128), F32)
        dv = jnp.zeros((T, 128), F32)
        for hh in range(2):
            n = 2 * g + hh
            q = only(query, hh)
            d = only(do[g, mid_rows, :], hh)
            m, inv = ml_ref[0, n], ml_ref[1, n]
            s = nt(kv_ref[0, g], q)
            dp = nt(kv_ref[1, g], d)
            p0 = jnp.exp(s[:T] - (m - up_bias)) * inv
            p1 = jnp.exp(s[T : 2 * T] - m) * inv
            p2 = jnp.exp(s[2 * T :] - (m - down_bias)) * inv
            p = jnp.concatenate([p0, p1, p2], axis=0)
            row = jnp.sum(p * dp, axis=0, keepdims=True)
            delta[n] = row
            ds = (p * (dp - row)).astype(BF)
            parts.append(nn(t_ref[0, g, pl.ds(hh * HD, HD), :], ds) * 0.125)
            dk = dk + nn(ds[T : 2 * T], q)
            dv = dv + nn(p1.astype(BF), d)
        dq[g] = jnp.transpose(jnp.concatenate(parts, axis=0)).astype(BF)
        dkv[0, g] = dk
        dkv[1, g] = dv
        return carry

    lax.fori_loop(0, G, own, 0)
    start, wait = swap_rows(delta, delta_h.at[0], delta_h.at[1], s_d, r_d)
    start()
    wait()
    gn[...] = jnp.zeros_like(gn)

    def other(g, carry):
        dk = dkv[0, g]
        dv = dkv[1, g]
        for side in range(2):
            rows = pl.ds(side * 2 * T, T)
            query = q_ref[g, rows, :] * jnp.asarray(0.125, BF)
            for hh in range(2):
                n = 2 * g + hh
                q = only(query, hh)
                d = only(do[g, rows, :], hh)
                s = nt(kv_ref[0, g, mid_rows, :], q)
                dp = nt(kv_ref[1, g, mid_rows, :], d)
                p = jnp.exp(s - mlh_ref[side, 0, n]) * mlh_ref[side, 1, n]
                ds = (p * (dp - delta_h[side, n])).astype(BF)
                dk = dk + nn(ds, q)
                dv = dv + nn(p.astype(BF), d)
        three = jnp.concatenate([dq[g], dk.astype(BF), dv.astype(BF)], axis=1)
        gn[...] += nt(three, w_ref[g]).astype(BF).astype(F32)
        return carry

    lax.fori_loop(0, G, other, 0)
    hat, inv = moments(wide(x_ref, 1).astype(F32))
    grad_hat = gn[...] * gain[...]
    mean = jnp.sum(grad_hat, axis=-1, keepdims=True) * (1.0 / D)
    cross = jnp.sum(grad_hat * hat, axis=-1, keepdims=True) * (1.0 / D)
    total = (gu[...] + (grad_hat - mean - hat * cross) * inv).astype(BF)
    for g in range(G):
        outgo[g] = total[:, g * 128 : (g + 1) * 128]
    here = (r, pl.ds(w * T, T))
    sends = []
    for i in range(1, G):
        dev = chan_peer(i)
        copy = remote(outgo.at[dev[1]], back.at[here[0], here[1]], s_y.at[i], r_y.at[i], dev)
        copy.start()
        sends.append(copy)
    back[here[0], here[1], :] = outgo[c]
    for copy in sends:
        copy.wait()


def backward(x, gain, w, wo, dec, q, kv, t, ml, mlh, gf):
    scratch = [
        pltpu.VMEM((T, D), F32),
        pltpu.VMEM((3 * T, D), BF),
        pltpu.VMEM((G, 3 * T, 128), BF),
        pltpu.VMEM((G, T, 128), BF),
        pltpu.VMEM((2, G, T, 128), F32),
        pltpu.VMEM((16, 1, T), F32),
        pltpu.VMEM((2, 16, 1, T), F32),
        pltpu.VMEM((T, D), F32),
        pltpu.VMEM((G, T, 128), BF),
        DMA((2,)), DMA((2,)), DMA((G,)), DMA((G,)),
    ]
    return call(
        backward_kernel, sds((4, 512, 128), BF), [VM] * 11, VM, scratch, 3, "backward",
        (x, gain, w, wo, dec, q, kv, t, ml, mlh, gf),
    )


def body(state, background, gain, w_query, w_key, w_value, w_out, decoder, interp, obs_values, tile_index, block_count):
    w3 = jnp.concatenate([w_query, w_key, w_value], axis=1)
    dec = jnp.pad(jnp.transpose(decoder), ((0, VP - VARS), (0, 0)))
    idx = jnp.broadcast_to(tile_index.reshape(L, 16, 1), (L, 16, 128))
    x, w, wo, dec, idx = gather(state, w3, w_out, dec, idx)
    gain = gain.reshape(1, D)
    q, kv, t, ml, f = forward(x, gain, w, wo, dec)
    mlh, picked = pick(f, ml, idx)
    am = observe(block_count.reshape(L), picked, interp.reshape(L, 16, 128, 128), obs_values.reshape(L, 16, 128))
    misfit, gf = settle(am, idx)
    back = backward(x, gain, w, wo, dec, q, kv, t, ml, mlh, gf)
    gradient = state.astype(F32) - background.astype(F32) + back.astype(F32)
    return misfit.reshape(L, 1, 1, 16, 128), gradient


def solution(mesh):
    return jax.shard_map(
        body,
        mesh=mesh,
        in_specs=(
            P("lat", None, "chan"),
            P("lat", None, "chan"),
            P(),
            P(None, "chan"),
            P(None, "chan"),
            P(None, "chan"),
            P("chan", None),
            P("chan", None),
            P("lat", "chan", None, None, None, None),
            P("lat", "chan", None, None, None),
            P("lat", "chan", None, None),
            P("lat", "chan", None),
        ),
        out_specs=(P(None, "chan", "lat", None, None), P("lat", None, "chan")),
        check_vma=False,
    )
```

time: 629 us -> 252 us (0.40); the launches traced: 622 us -> 252 us
  Pallas kernels: 0 us -> 244 us
  waiting for transfers between devices: 220 us -> 0 us
  matrix products: 139 us -> 0 us
  blocking collectives: 96.8 us -> 0 us
  local copies, waits for them, and re-layouts: 73.5 us -> 2.92 us
  starting transfers between devices: 42.3 us -> 0 us
  other arithmetic: 36.7 us -> 4.32 us
  between operations: 14.7 us -> 0.72 us
    pallas_call x0 -> x6, Pallas kernels: none -> 244 us  [the longest x5 217 us: call(): pl.pallas_call(kernel, out_shape=out_shape, in_specs=in_specs, out_specs=...]
    dot_general x17 -> x0, matrix products: 128 us -> none  [the longest x1 40.1 us: attend_backward(): jnp.einsum('rwhij,rwihd->rwjhd', grad_scores, queries, preferred_element_...]
    all_gather x2 -> x0, waiting for transfers between devices: 115 us -> none  [the longest x1 61.4 us: body(): wide_state = lax.all_gather(state, 'chan', axis=2, tiled=True)]
    all_to_all x3 -> x0, blocking collectives: 96.8 us -> none  [the longest x1 52 us: sent_and_summed(): lax.all_to_all(in_blocks(array, dim, length), axis, 0, 0, tiled=True)]
    unnamed x4 -> x0, waiting for transfers between devices: 53.2 us -> none
    all_to_all x4 -> x0, waiting for transfers between devices: 45.8 us -> none  [the longest x1 29.8 us: from_everyone(): return lax.all_to_all(copies, axis, split_axis=0, concat_axis=0, tiled=True)]
    reshape x15 -> x0, local copies, waits for them, and re-layouts: 36.3 us -> none  [the longest x2 9.17 us: unwindow(): shaped = windowed.reshape(rows_band, NC // WC, 3, WC, width_heads)]
    all_to_all x4 -> x0, starting transfers between devices: 21.6 us -> none  [the longest x1 8.45 us: body(): lax.all_to_all(tile_index, 'lat', split_axis=2, concat_axis=0, tiled=True)]
  transfers between devices with their start and end apart: 11 -> 0, of which waited for: 8 -> 0; matrix products, arithmetic and copies ran while one was open for 4% -> 0% of each run, Pallas kernels for 0% -> 0%
where the time goes in v1:
time: 252 us
  Pallas kernels  244 us (97%)
  other arithmetic  4.32 us (2%)
  local copies, waits for them, and re-layouts  2.92 us (1%)
    pallas_call x5, Pallas kernels, call(): pl.pallas_call(kernel, out_shape=out_shape, in_specs=in_specs, out_specs=...  217 us
    pallas_call x1, Pallas kernels, observe(): pl.pallas_call(observe_kernel, out_shape=sds((L, 32, 128), BF), grid_spec...  27.4 us

profile of v1, /device:TPU:1, one launch (start us, length us, event | category | flops | bytes accessed | tf_op | source)
XLA Modules:
  0.0 252.4 jit_solution(3010581187745549820)
XLA Ops:
  0.6 0.0 copy-start.3
  0.6 0.0 copy-start.4
  0.7 2.1 pad_maximum_fusion.w3
  2.8 0.0 copy-done.3
  2.8 0.6 pad.4.dec
  3.4 0.0 copy-done.4
  3.4 0.8 broadcast_in_dim.11.idx
  4.1 0.9 broadcast_in_dim.12.zero
  5.0 89.5 %gather.1 = (bf16[3,8,256,128]{3,2,1,0:T(8,128)(2,1)}, bf16[8,1024,384]{2,1,0:T(8,128)(2,1)}, bf16[8,128,1024]{2,1,0:T(8,128)(2,1)}, bf16[8,80,128]{2,1,0:T(8,128)(2,1)}, s32[16,16,128]{2,1,0:T(8,128)}) custom-call(bf16[4,512,128]{2,1,0:T(8,128)(2,1)} %state.1, bf16[1024,384]{1,0:T(8,128)(2,1)} %pad_maximum_fusion.w3, bf16[128,1024]{1,0:T(8,128)(2,1)} %wo.1, ...), custom_call_target="tpu_custom_call" | custom-call | tf_op jit(solution)/shard_map/gather/pallas_call | solution.py:88
  94.5 28.5 %forward.1 = (bf16[8,768,128]{2,1,0:T(8,128)(2,1)}, bf16[2,8,768,128]{3,2,1,0:T(8,128)(2,1)}, bf16[2,8,128,768]{3,2,1,0:T(8,128)(2,1)}, f32[2,16,1,256]{3,2,1,0:T(1,128)}, bf16[80,256]{1,0:T(8,128)(2,1)}) custom-call(bf16[3,8,256,128]{3,2,1,0:T(8,128)(2,1)} %get-tuple-element.16.x_ref, f32[1,1024]{1,0:T(1,128)} %bitcast.13, ...), custom_call_target="tpu_custom_call" | custom-call | tf_op jit(solution)/shard_map/forward/pallas_call | solution.py:88
  123.0 22.0 %pick.1 = (f32[2,2,16,1,256]{4,3,2,1,0:T(1,128)}, bf16[16,16,128]{2,1,0:T(8,128)(2,1)}) custom-call(bf16[80,256]{1,0:T(8,128)(2,1)} %get-tuple-element.20.f_ref, f32[2,16,1,256]{3,2,1,0:T(1,128)} %get-tuple-element.21.ml_ref, s32[16,16,128]{2,1,0:T(8,128)} %get-tuple-element.22.idx_ref), custom_call_target="tpu_custom_call" | custom-call | tf_op jit(solution)/shard_map/pick/pallas_call | solution.py:88
  144.9 27.4 %observe.1.am = bf16[16,32,128]{2,1,0:T(8,128)(2,1)} custom-call(s32[16]{0:T(128)} %bitcast.16, bf16[16,16,128]{2,1,0:T(8,128)(2,1)} %get-tuple-element.23.picked, bf16[16,16,128,128]{3,2,1,0:T(8,128)(2,1)} %bitcast.9, bf16[16,16,128]{2,1,0:T(8,128)(2,1)} %bitcast.11), custom_call_target="tpu_custom_call" | custom-call | tf_op jit(solution)/shard_map/observe/pallas_call | solution.py:424
  172.3 27.6 %settle.1 = (f32[16,16,128]{2,1,0:T(8,128)}, f32[3,80,256]{2,1,0:T(8,128)}) custom-call(bf16[16,32,128]{2,1,0:T(8,128)(2,1)} %observe.1.am, s32[16,16,128]{2,1,0:T(8,128)} %get-tuple-element.22.idx_ref), custom_call_target="tpu_custom_call" | custom-call | tf_op jit(solution)/shard_map/settle/pallas_call | solution.py:88
  199.9 0.0 copy-start
  200.0 0.0 copy-start.1
  200.0 49.5 %backward.1 = bf16[4,512,128]{2,1,0:T(8,128)(2,1)} custom-call(bf16[3,8,256,128]{3,2,1,0:T(8,128)(2,1)} %get-tuple-element.16.x_ref, f32[1,1024]{1,0:T(1,128)} %bitcast.14, bf16[8,1024,384]{2,1,0:T(8,128)(2,1)} %get-tuple-element.17.w_ref, bf16[8,128,1024]{2,1,0:T(8,128)(2,1)} %get-tuple-element.18.wo_ref, bf16[8,80,128]{2,1,0:T(8,128)(2,1)} %get-tuple-element.19.dec_ref, ...), custom_call_target="tpu_custom_call" | custom-call | tf_op jit(solution)/shard_map/backward/pallas_call | solution.py:88
  249.4 0.0 copy-done
  249.5 0.0 copy-done.1
  249.5 0.0 copy-start.2
  249.5 2.2 convert_add_fusion
  251.7 0.0 copy-done.2
  251.7 0.7 copy.16
Async XLA Ops:
  0.6 2.1 copy-start.3
  0.6 2.7 %copy-start.4 = (s32[1,1,16,16]{3,2,1,0:T(8,128)S(1)}, s32[1,1,16,16]{3,2,1,0:T(8,128)}, u32[]{:S(2)}) copy-start(s32[1,1,16,16]{3,2,1,0:T(8,128)} %param.22) | copy-start | bytes 3076
  199.9 49.5 %copy-start = (bf16[4,512,128]{2,1,0:T(8,128)(2,1)S(1)}, bf16[4,512,128]{2,1,0:T(8,128)(2,1)}, u32[]{:S(2)}) copy-start(bf16[4,512,128]{2,1,0:T(8,128)(2,1)} %state.1) | copy-start | bytes 1572868
  200.0 49.5 %copy-start.1 = (bf16[4,512,128]{2,1,0:T(8,128)(2,1)S(1)}, bf16[4,512,128]{2,1,0:T(8,128)(2,1)}, u32[]{:S(2)}) copy-start(bf16[4,512,128]{2,1,0:T(8,128)(2,1)} %param.13) | copy-start | bytes 1572868
  249.5 2.2 copy-start.2

commit v2 on v1

v2 whole, which is shorter than its diff:
```python
import functools

import jax
import jax.numpy as jnp
from jax import lax
from jax.experimental import pallas as pl
from jax.experimental.pallas import tpu as pltpu
from jax.sharding import PartitionSpec as P

D = 1024
HD = 64
VARS = 69
EPSILON = 1e-05
VP = 80
T = 256
G = 8
L = 16
BIG = 1e30
MESH = pl.DeviceIdType.MESH
BF = jnp.bfloat16
F32 = jnp.float32
VMEM_LIMIT = 62 * 1024 * 1024


def nn(a, b):
    return lax.dot_general(a, b, (((1,), (0,)), ((), ())), preferred_element_type=F32)


def nt(a, b):
    return lax.dot_general(a, b, (((1,), (1,)), ((), ())), preferred_element_type=F32)


def place():
    b = lax.axis_index("lat")
    c = lax.axis_index("chan")
    k = b % 2
    x = c % 4
    r = x + k * (3 - 2 * x)
    return b, c, r, c // 4, k


def row_of(c, k):
    x = c % 4
    return x + k * (3 - 2 * x)


def neighbours():
    b, c, r, w, k = place()
    inner_up = (r > 0).astype(jnp.int32)
    inner_down = (r < 3).astype(jnp.int32)
    up = (b - 1 + inner_up, c + inner_up * (2 * k - 1))
    down = (b + 1 - inner_down, c + inner_down * (1 - 2 * k))
    row = b * 4 + r
    return up, down, row > 0, row < 4 * L - 1


def chan_peer(i):
    b, c, _, _, _ = place()
    return (b, (c + i) % G)


def lat_peer(i):
    b, c, _, _, _ = place()
    return ((b + i) % L, c)


def greet(chan=True, lat=False, rows=False):
    barrier = pltpu.get_barrier_semaphore()
    count = 0
    if chan:
        for i in range(1, G):
            pl.semaphore_signal(barrier, inc=1, device_id=chan_peer(i), device_id_type=MESH)
            count += 1
    if lat:
        for i in range(1, L):
            pl.semaphore_signal(barrier, inc=1, device_id=lat_peer(i), device_id_type=MESH)
            count += 1
    pl.semaphore_wait(barrier, count)


def remote(src, dst, ss, rs, dev):
    return pltpu.make_async_remote_copy(
        src_ref=src, dst_ref=dst, send_sem=ss, recv_sem=rs, device_id=dev, device_id_type=MESH
    )


def call(kernel, out_shape, in_specs, out_specs, scratch, cid, name, args):
    return pl.pallas_call(
        kernel,
        out_shape=out_shape,
        in_specs=in_specs,
        out_specs=out_specs,
        scratch_shapes=scratch,
        compiler_params=pltpu.CompilerParams(
            collective_id=cid, has_side_effects=cid is not None, vmem_limit_bytes=VMEM_LIMIT
        ),
        name=name,
    )(*args)


VM = pl.BlockSpec(memory_space=pltpu.VMEM)
ANY = pl.BlockSpec(memory_space=pl.ANY)
DMA = pltpu.SemaphoreType.DMA


def sds(shape, dtype):
    return jax.ShapeDtypeStruct(shape, dtype)


class Spread:
    def __init__(self, view, size, sems):
        self.view, self.size = view, size
        self.s1, self.r1, self.s2, self.s3, self.r3, self.s4, self.r4, self.s5, self.r5 = sems
        b, c, _, z, k = place()
        x, y = c % 4, b // 4
        p = y % 2
        self.b, self.c, self.x, self.z = b, c, x, z
        self.start = (p * 2 + k) * size
        self.across = ((1 - p) * 2 + k) * size
        self.core = (b + 1 - 2 * k, c)
        self.ups = [((b + 4) % L, c), ((b + 12) % L, c)]
        self.flip = (b, (c + 4) % G)
        self.sent = []

    def send(self, g, start, size, ss, rs, dev):
        ref = self.view(g, start, size)
        copy = remote(ref, ref, ss, rs, dev)
        copy.start()
        self.sent.append(copy)

    def wait(self, g, start, size, rs):
        ref = self.view(g, start, size)
        remote(ref, ref, self.s1.at[0], rs, self.core).wait_recv()

    def from_x(self, i):
        return self.z * 4 + (self.x + 4 - i) % 4

    def from_z(self, i):
        return (1 - self.z) * 4 + (self.x + 4 - i) % 4

    def others(self):
        return [self.from_x(i) for i in (1, 3, 2)] + [self.from_z(i) for i in (0, 1, 3, 2)]

    def first(self):
        c = self.c
        self.send(c, self.start, self.size, self.s1.at[0], self.r1.at[c], self.flip)
        for i in (1, 3, 2):
            dev = (self.b, self.z * 4 + (self.x + i) % 4)
            self.send(c, self.start, self.size, self.s1.at[i], self.r1.at[c], dev)

    def fan(self, g):
        half = self.size // 2
        for h in range(2):
            self.send(g, self.start + h * half, half, self.s4.at[h, g], self.r4.at[h, g], self.ups[h])
        self.send(g, self.start, self.size, self.s3.at[g], self.r3.at[g], self.core)

    def relay_x(self):
        for i in (1, 3, 2):
            g = self.from_x(i)
            self.wait(g, self.start, self.size, self.r1.at[g])
            self.send(g, self.start, self.size, self.s2.at[i], self.r1.at[g], self.flip)
            self.fan(g)

    def relay_z(self):
        for i in (0, 1, 3, 2):
            g = self.from_z(i)
            self.wait(g, self.start, self.size, self.r1.at[g])
            self.fan(g)

    def relay_y(self):
        half = self.size // 2
        for g in self.others():
            for h in range(2):
                start = self.across + h * half
                self.wait(g, start, half, self.r4.at[h, g])
                self.send(g, start, half, self.s5.at[h, g], self.r5.at[h, g], self.core)

    def ready(self):
        half = self.size // 2
        _, _, _, _, k = place()
        turn = (1 - 2 * k) * self.size
        for g in self.others():
            self.wait(g, self.start + turn, self.size, self.r3.at[g])
            for h in range(2):
                self.wait(g, self.across + turn + h * half, half, self.r5.at[h, g])

    def finish(self):
        for copy in self.sent:
            copy.wait_send()


def wide(ref, h):
    return jnp.concatenate([ref[h, g] for g in range(G)], axis=1)


def moments(x):
    mean = jnp.sum(x, axis=-1, keepdims=True) * (1.0 / D)
    centred = x - mean
    var = jnp.sum(centred * centred, axis=-1, keepdims=True) * (1.0 / D)
    inv = lax.rsqrt(var + EPSILON)
    return centred * inv, inv


def only(value, hh):
    first = lax.broadcasted_iota(jnp.int32, value.shape, 1) < HD
    keep = first if hh == 0 else jnp.logical_not(first)
    return jnp.where(keep, value, jnp.zeros_like(value))


def swap_rows(src, above, below, ss, rs):
    up, down, has_up, has_down = neighbours()
    to_up = remote(src, below, ss.at[0], rs.at[0], up)
    to_down = remote(src, above, ss.at[1], rs.at[1], down)

    def start():
        pl.when(has_up)(lambda: to_up.start())
        pl.when(has_down)(lambda: to_down.start())

    def wait():
        @pl.when(has_up)
        def _():
            to_up.wait_send()
            to_down.wait_recv()

        @pl.when(has_down)
        def _():
            to_down.wait_send()
            to_up.wait_recv()

    return start, wait


def run_of(c, half, k):
    return row_of(c, k) * 4 + (c // 4) * 2 + half


def loop(n, step):
    def wrapped(i, carry):
        step(i)
        return carry

    lax.fori_loop(0, n, wrapped, 0)


SCRATCH = dict(
    x_v=pltpu.VMEM((3, G, T, 128), BF),
    w_v=pltpu.VMEM((G, 3, D, 128), BF),
    o_v=pltpu.VMEM((G, 128, D), BF),
    d_v=pltpu.VMEM((G, VP, 128), BF),
    i_v=pltpu.VMEM((L, 16, 128), jnp.int32),
    itp=pltpu.VMEM((L, 16, 128, 128), BF),
    n_v=pltpu.VMEM((3 * T, D), BF),
    qkv=pltpu.VMEM((3, G, 3 * T, 128), BF),
    kt=pltpu.VMEM((G, 128, 3 * T), BF),
    mix=pltpu.VMEM((G, T, 128), BF),
    acc=pltpu.VMEM((T, D), F32),
    ml=pltpu.VMEM((2, 16, 1, T), F32),
    mlh=pltpu.VMEM((2, 2, 16, 1, T), F32),
    fields=pltpu.VMEM((G, VP, T), BF),
    mine=pltpu.VMEM((L, 16, 128), BF),
    picked=pltpu.VMEM((L, 16, 128), BF),
    am=pltpu.VMEM((L, 32, 128), BF),
    came=pltpu.VMEM((L, 32, 128), BF),
    parts=pltpu.VMEM((G, VP, T), BF),
    got=pltpu.VMEM((G, VP, T), BF),
    gf=pltpu.VMEM((3, VP, T), F32),
    gu=pltpu.VMEM((T, D), F32),
    low=pltpu.VMEM((3 * T, D), BF),
    do=pltpu.VMEM((G, 3 * T, 128), BF),
    dq=pltpu.VMEM((G, T, 128), BF),
    dkv=pltpu.VMEM((2, G, T, 128), F32),
    delta=pltpu.VMEM((16, 1, T), F32),
    delta_h=pltpu.VMEM((2, 16, 1, T), F32),
    outgo=pltpu.VMEM((G, T, 128), BF),
    loc=DMA((8,)),
    s_state=DMA((G,)), r_state=DMA((G,)),
    s_d=DMA((G,)), r_d=DMA((G,)),
    s_i=DMA((L,)), r_i=DMA((L,)),
    s_h=DMA((2, G)), r_h=DMA((2, G)),
    s_f=DMA((G,)), r_f=DMA((G,)),
    s_p=DMA((L,)), r_p=DMA((L,)),
    s_a=DMA((L,)), r_a=DMA((L,)),
    s_g=DMA((G,)), r_g=DMA((G,)),
    s_y=DMA((G,)), r_y=DMA((G,)),
    s_m=DMA((2,)), r_m=DMA((2,)),
    s_gh=DMA((2,)), r_gh=DMA((2,)),
    s_dl=DMA((2, 2)), r_dl=DMA((2, 2)),
    w1=DMA((4,)), w2=DMA((G,)), w3=DMA((4,)), w4=DMA((G,)), w5=DMA((G,)), w6=DMA((2, G)), w7=DMA((2, G)), w8=DMA((2, G)), w9=DMA((2, G)),
    o1=DMA((4,)), o2=DMA((G,)), o3=DMA((4,)), o4=DMA((G,)), o5=DMA((G,)), o6=DMA((2, G)), o7=DMA((2, G)), o8=DMA((2, G)), o9=DMA((2, G)),
)


class Refs:
    pass


def kernel(state, wq, wk, wv, wo, dec, idx, gain, interp, obs, count, misfit, back, *scratch):
    s = Refs()
    for name, ref in zip(SCRATCH, scratch):
        setattr(s, name, ref)
    b, c, r, w, k = place()
    up, down, has_up, has_down = neighbours()
    up_bias = jnp.where(has_up, 0.0, -BIG).astype(F32)
    down_bias = jnp.where(has_down, 0.0, -BIG).astype(F32)
    mid_rows = pl.ds(T, T)
    eighth = jnp.asarray(0.125, BF)

    local = [
        pltpu.make_async_copy(state.at[r, pl.ds(w * T, T)], s.x_v.at[1, c], s.loc.at[0]),
        pltpu.make_async_copy(wq, s.w_v.at[c, 0], s.loc.at[1]),
        pltpu.make_async_copy(wk, s.w_v.at[c, 1], s.loc.at[2]),
        pltpu.make_async_copy(wv, s.w_v.at[c, 2], s.loc.at[3]),
        pltpu.make_async_copy(wo, s.o_v.at[c], s.loc.at[4]),
        pltpu.make_async_copy(dec, s.d_v.at[c], s.loc.at[5]),
        pltpu.make_async_copy(idx.at[b], s.i_v.at[b], s.loc.at[6]),
        pltpu.make_async_copy(interp, s.itp, s.loc.at[7]),
    ]
    for copy in local:
        copy.start()

    @pl.when(jnp.logical_not(has_up))
    def _():
        s.x_v[0] = jnp.zeros((G, T, 128), BF)

    @pl.when(jnp.logical_not(has_down))
    def _():
        s.x_v[2] = jnp.zeros((G, T, 128), BF)

    s.mlh[:, 0] = jnp.full((2, 16, 1, T), BIG, F32)
    s.mlh[:, 1] = jnp.zeros((2, 16, 1, T), F32)
    s.delta_h[...] = jnp.zeros_like(s.delta_h)
    s.gf[...] = jnp.zeros_like(s.gf)
    greet(chan=True, lat=True)

    sends = []
    states = {}
    for i in (1, 3, 4, 5, 7, 2, 6):
        _, pc = chan_peer(i)
        pr = row_of(pc, k)
        copy = remote(state.at[pr, pl.ds((pc // 4) * T, T)], s.x_v.at[1, c], s.s_state.at[i], s.r_state.at[i], (b, pc))
        copy.start()
        sends.append(copy)
        states[i] = copy
    weights = Spread(
        lambda g, at, n: s.w_v.at[g, :, pl.ds(at, n)], 256, (s.w1, s.w2, s.w3, s.w4, s.w5, s.w6, s.w7, s.w8, s.w9)
    )
    outs = Spread(
        lambda g, at, n: s.o_v.at[g, pl.ds(at, n)], 32, (s.o1, s.o2, s.o3, s.o4, s.o5, s.o6, s.o7, s.o8, s.o9)
    )
    for copy in local[1:4]:
        copy.wait()
    weights.first()
    for i in range(1, L):
        dev = lat_peer(i)
        copy = remote(idx.at[dev[0]], s.i_v.at[b], s.s_i.at[i], s.r_i.at[i], dev)
        copy.start()
        sends.append(copy)

    def halo(g, sem):
        to_up = remote(s.x_v.at[1, g], s.x_v.at[2, g], s.s_h.at[0, sem], s.r_h.at[0, sem], up)
        to_down = remote(s.x_v.at[1, g], s.x_v.at[0, g], s.s_h.at[1, sem], s.r_h.at[1, sem], down)
        return to_up, to_down

    def start_halo(g, sem):
        to_up, to_down = halo(g, sem)
        pl.when(has_up)(lambda: to_up.start())
        pl.when(has_down)(lambda: to_down.start())

    local[0].wait()
    start_halo(c, 0)
    for i in (1, 3, 4, 5, 7, 2, 6):
        states[i].wait_recv()
        start_halo((c + G - i) % G, i)
    weights.relay_x()
    local[4].wait()
    outs.first()
    for i in range(1, G):
        copy = remote(dec, s.d_v.at[c], s.s_d.at[i], s.r_d.at[i], chan_peer(i))
        copy.start()
        sends.append(copy)

    def norm(h):
        hat, _ = moments(wide(s.x_v, h).astype(F32))
        s.n_v[pl.ds(h * T, T), :] = (hat * gain[...]).astype(BF)

    norm(1)
    weights.relay_z()
    weights.relay_y()
    for i in range(G):
        to_up, to_down = halo((c + G - i) % G, i)
        pl.when(has_down)(lambda: to_up.wait_recv())
        pl.when(has_up)(lambda: to_down.wait_recv())
    norm(0)
    norm(2)
    weights.ready()

    def project(g):
        res = nn(s.n_v[...], jnp.concatenate([s.w_v[g, 0], s.w_v[g, 1], s.w_v[g, 2]], axis=1))
        for i in range(3):
            s.qkv[i, g] = res[:, i * 128 : (i + 1) * 128].astype(BF)
        s.kt[g] = jnp.transpose(res[:, 128:256]).astype(BF)

    loop(G, project)

    def attend(g):
        query = s.qkv[0, g, mid_rows, :] * eighth
        vt = jnp.transpose(s.qkv[2, g].astype(F32)).astype(BF)
        parts = []
        for hh in range(2):
            q = only(query, hh)
            sc = nt(s.qkv[1, g], q)
            m0 = jnp.max(sc[:T], axis=0, keepdims=True) + up_bias
            m1 = jnp.max(sc[T : 2 * T], axis=0, keepdims=True)
            m2 = jnp.max(sc[2 * T :], axis=0, keepdims=True) + down_bias
            m = jnp.maximum(jnp.maximum(m0, m1), m2)
            e0 = jnp.exp(sc[:T] - (m - up_bias))
            e1 = jnp.exp(sc[T : 2 * T] - m)
            e2 = jnp.exp(sc[2 * T :] - (m - down_bias))
            l = jnp.sum(e0, axis=0, keepdims=True) + jnp.sum(e1, axis=0, keepdims=True) + jnp.sum(e2, axis=0, keepdims=True)
            inv = 1.0 / l
            p = jnp.concatenate([(e0 * inv).astype(BF), (e1 * inv).astype(BF), (e2 * inv).astype(BF)], axis=0)
            parts.append(nn(vt[hh * HD : (hh + 1) * HD], p))
            s.ml[0, 2 * g + hh] = m
            s.ml[1, 2 * g + hh] = inv
        s.mix[g] = jnp.transpose(jnp.concatenate(parts, axis=0)).astype(BF)

    loop(2, attend)
    outs.relay_x()
    loop(2, lambda g: attend(g + 2))
    outs.relay_z()
    loop(2, lambda g: attend(g + 4))
    outs.relay_y()
    loop(2, lambda g: attend(g + 6))
    start_ml, wait_ml = swap_rows(s.ml, s.mlh.at[0], s.mlh.at[1], s.s_m, s.r_m)
    start_ml()
    outs.ready()
    local[5].wait()
    for i in range(1, G):
        remote(dec, s.d_v.at[0], s.s_d.at[i], s.r_d.at[i], chan_peer(i)).wait_recv()
    s.acc[...] = wide(s.x_v, 1).astype(F32) * 0.0

    def out(g):
        s.acc[...] += nn(s.mix[g], s.o_v[g]).astype(BF).astype(F32)

    loop(G, out)
    updated = (wide(s.x_v, 1).astype(F32) + s.acc[...]).astype(BF)
    dec_all = jnp.concatenate([s.d_v[g] for g in range(G)], axis=1)
    s.fields[c] = nt(dec_all, updated).astype(BF)

    copies = []
    for i in range(1, G):
        copy = remote(s.fields.at[c], s.fields.at[c], s.s_f.at[i], s.r_f.at[i], chan_peer(i))
        copy.start()
        copies.append(copy)
        sends.append(copy)
    local[6].wait()
    for i in range(1, L):
        remote(idx.at[0], s.i_v.at[0], s.s_i.at[i], s.r_i.at[i], lat_peer(i)).wait_recv()
    index = s.i_v[...].reshape(16 * L, 128)
    lanes = lax.broadcasted_iota(jnp.int32, (16 * L, 128), 1) * 16

    def one(g, total):
        for half in range(2):
            hot = (index == lanes + run_of(g, half, k)).astype(F32).astype(BF)
            total = total + nn(hot[:, :VP], s.fields[g, :, pl.ds(half * 128, 128)])
        return total

    total = one(c, jnp.zeros((16 * L, 128), F32))
    for i in range(1, G):
        copies[i - 1].wait_recv()
        total = one((c + G - i) % G, total)
    s.mine[...] = total.astype(BF).reshape(L, 16, 128)
    for i in range(1, L):
        dev = lat_peer(i)
        copy = remote(s.mine.at[dev[0]], s.picked.at[b], s.s_p.at[i], s.r_p.at[i], dev)
        copy.start()
        sends.append(copy)
    s.picked[b] = s.mine[b]

    local[7].wait()
    row = lax.broadcasted_iota(jnp.int32, (16, 128), 0)

    def observe(i):
        band = (b + L - i) % L

        @pl.when(i > 0)
        def _():
            remote(s.mine.at[b], s.picked.at[b], s.s_p.at[i], s.r_p.at[i], (band, c)).wait_recv()

        flat = s.itp[band].reshape(2048, 128)
        big = nt(s.picked[band], flat)
        pred = jnp.zeros((16, 128), F32)
        for n in range(16):
            pred = jnp.where(row == n, big[:, n * 128 : (n + 1) * 128], pred)
        mis = jnp.where(row < count[band], pred - obs[band].astype(F32), 0.0).astype(BF)
        lhs = jnp.concatenate([jnp.where(row == n, mis, jnp.zeros_like(mis)) for n in range(16)], axis=1)
        s.am[band, :16, :] = nn(lhs, flat).astype(BF)
        s.am[band, 16:, :] = mis

        @pl.when(i > 0)
        def _():
            remote(s.am.at[band], s.came.at[b], s.s_a.at[i], s.r_a.at[i], (band, c)).start()

    loop(L, observe)
    s.came[b] = s.am[b]

    index_t = jnp.transpose(index.astype(F32))[:VP].astype(jnp.int32)
    sub = lax.broadcasted_iota(jnp.int32, (VP, 16 * L), 0) * 16

    def arrived(i):
        band = (b + i) % L

        @pl.when(i > 0)
        def _():
            remote(s.am.at[b], s.came.at[b], s.s_a.at[i], s.r_a.at[i], (band, c)).wait()

    loop(L, arrived)
    misfit[...] = s.came[:, 16:, :].astype(F32)
    adjoint = s.came[:, :16, :].reshape(16 * L, 128)
    reduce = []
    for i in list(range(1, G)) + [0]:
        g = (c + i) % G
        for half in range(2):
            hot = (index_t == sub + run_of(g, half, k)).astype(F32).astype(BF)
            s.parts[g, :, pl.ds(half * 128, 128)] = nn(hot, adjoint).astype(BF)
        if i:
            copy = remote(s.parts.at[g], s.got.at[c], s.s_g.at[i], s.r_g.at[i], (b, g))
            copy.start()
            reduce.append(copy)
            sends.append(copy)
    total = s.parts[c].astype(F32)
    for i in range(1, G):
        reduce[i - 1].wait_recv()
        total = total + s.got[(c + G - i) % G].astype(F32)
    s.gf[1] = total
    start_gf, wait_gf = swap_rows(s.gf.at[1], s.gf.at[0], s.gf.at[2], s.s_gh, s.r_gh)
    start_gf()
    wait_ml()

    dec_all = jnp.concatenate([dec_all, jnp.zeros((128 - VP, D), BF)], axis=0)
    dec3 = jnp.concatenate([dec_all, dec_all, dec_all], axis=0)

    def update_of(h):
        field = jnp.transpose(jnp.concatenate([s.gf[h], jnp.zeros((128 - VP, T), F32)], axis=0))
        hi = field.astype(BF)
        rest = field - hi.astype(F32)
        mid = rest.astype(BF)
        lo = (rest - mid.astype(F32)).astype(BF)
        update = nn(jnp.concatenate([hi, mid, lo], axis=1), dec3)
        s.low[pl.ds(h * T, T), :] = update.astype(BF)
        return update

    s.gu[...] = update_of(1)
    wait_gf()
    update_of(0)
    update_of(2)

    def mixed(g):
        s.do[g] = nt(s.low[...], s.o_v[g]).astype(BF)

    loop(G, mixed)

    def own(g):
        query = s.qkv[0, g, mid_rows, :] * eighth
        parts = []
        dk = jnp.zeros((T, 128), F32)
        dv = jnp.zeros((T, 128), F32)
        for hh in range(2):
            n = 2 * g + hh
            q = only(query, hh)
            d = only(s.do[g, mid_rows, :], hh)
            m, inv = s.ml[0, n], s.ml[1, n]
            sc = nt(s.qkv[1, g], q)
            dp = nt(s.qkv[2, g], d)
            p0 = jnp.exp(sc[:T] - (m - up_bias)) * inv
            p1 = jnp.exp(sc[T : 2 * T] - m) * inv
            p2 = jnp.exp(sc[2 * T :] - (m - down_bias)) * inv
            p = jnp.concatenate([p0, p1, p2], axis=0)
            along = jnp.sum(p * dp, axis=0, keepdims=True)
            s.delta[n] = along
            ds = (p * (dp - along)).astype(BF)
            parts.append(nn(s.kt[g, pl.ds(hh * HD, HD), :], ds) * 0.125)
            dk = dk + nn(ds[T : 2 * T], q)
            dv = dv + nn(p1.astype(BF), d)
        s.dq[g] = jnp.transpose(jnp.concatenate(parts, axis=0)).astype(BF)
        s.dkv[0, g] = dk
        s.dkv[1, g] = dv

    def other(g):
        dk = s.dkv[0, g]
        dv = s.dkv[1, g]
        for side in range(2):
            rows = pl.ds(side * 2 * T, T)
            query = s.qkv[0, g, rows, :] * eighth
            for hh in range(2):
                n = 2 * g + hh
                q = only(query, hh)
                d = only(s.do[g, rows, :], hh)
                sc = nt(s.qkv[1, g, mid_rows, :], q)
                dp = nt(s.qkv[2, g, mid_rows, :], d)
                p = jnp.exp(sc - s.mlh[side, 0, n]) * s.mlh[side, 1, n]
                ds = (p * (dp - s.delta_h[side, n])).astype(BF)
                dk = dk + nn(ds, q)
                dv = dv + nn(p.astype(BF), d)
        three = jnp.concatenate([s.dq[g], dk.astype(BF), dv.astype(BF)], axis=1)
        wide_w = jnp.concatenate([s.w_v[g, 0], s.w_v[g, 1], s.w_v[g, 2]], axis=1)
        s.acc[...] += nt(three, wide_w).astype(BF).astype(F32)

    swaps = []
    for n in range(2):
        loop(4, lambda g: own(g + 4 * n))
        heads = pl.ds(8 * n, 8)
        start, wait = swap_rows(
            s.delta.at[heads], s.delta_h.at[0, heads], s.delta_h.at[1, heads], s.s_dl.at[n], s.r_dl.at[n]
        )
        start()
        swaps.append(wait)
    s.acc[...] = jnp.zeros_like(s.acc)
    for n in range(2):
        swaps[n]()
        loop(4, lambda g: other(g + 4 * n))

    hat, inv = moments(wide(s.x_v, 1).astype(F32))
    grad_hat = s.acc[...] * gain[...]
    mean = jnp.sum(grad_hat, axis=-1, keepdims=True) * (1.0 / D)
    cross = jnp.sum(grad_hat * hat, axis=-1, keepdims=True) * (1.0 / D)
    total = (s.gu[...] + (grad_hat - mean - hat * cross) * inv).astype(BF)
    for g in range(G):
        s.outgo[g] = total[:, g * 128 : (g + 1) * 128]
    here = pl.ds(w * T, T)
    final = []
    for i in range(1, G):
        dev = chan_peer(i)
        copy = remote(s.outgo.at[dev[1]], back.at[r, here], s.s_y.at[i], s.r_y.at[i], dev)
        copy.start()
        final.append(copy)
    back[r, here, :] = s.outgo[c]

    weights.finish()
    outs.finish()
    for copy in sends:
        copy.wait_send()
    for i in range(G):
        to_up, to_down = halo((c + G - i) % G, i)
        pl.when(has_up)(lambda: to_up.wait_send())
        pl.when(has_down)(lambda: to_down.wait_send())
    for copy in final:
        copy.wait()


def body(state, background, gain, w_query, w_key, w_value, w_out, decoder, interp, obs_values, tile_index, block_count):
    dec = jnp.pad(jnp.transpose(decoder), ((0, VP - VARS), (0, 0)))
    idx = jnp.broadcast_to(tile_index.reshape(L, 16, 1), (L, 16, 128))
    smem = pl.BlockSpec(memory_space=pltpu.SMEM)
    misfit, back = call(
        kernel,
        (sds((L, 16, 128), F32), sds((4, 512, 128), BF)),
        [ANY] * 7 + [VM, ANY, VM, smem],
        [VM] * 2,
        list(SCRATCH.values()),
        0,
        "whole",
        (
            state, w_query, w_key, w_value, w_out, dec, idx, gain.reshape(1, D),
            interp.reshape(L, 16, 128, 128), obs_values.reshape(L, 16, 128), block_count.reshape(L),
        ),
    )
    gradient = state.astype(F32) - background.astype(F32) + back.astype(F32)
    return misfit.reshape(L, 1, 1, 16, 128), gradient


def solution(mesh):
    return jax.shard_map(
        body,
        mesh=mesh,
        in_specs=(
            P("lat", None, "chan"),
            P("lat", None, "chan"),
            P(),
            P(None, "chan"),
            P(None, "chan"),
            P(None, "chan"),
            P("chan", None),
            P("chan", None),
            P("lat", "chan", None, None, None, None),
            P("lat", "chan", None, None, None),
            P("lat", "chan", None, None),
            P("lat", "chan", None),
        ),
        out_specs=(P(None, "chan", "lat", None, None), P("lat", None, "chan")),
        check_vma=False,
    )
```

time: 252 us -> 158 us (0.63)
  Pallas kernels: 244 us -> 150 us
    pallas_call x5 -> x1, Pallas kernels: 217 us -> 150 us  [call(): pl.pallas_call(kernel, out_shape=out_shape, in_specs=in_specs, out_specs=...]
    pallas_call x1 -> x0, Pallas kernels: 27.4 us -> none  [observe(): pl.pallas_call(observe_kernel, out_shape=sds((L, 32, 128), BF), grid_spec...]
where the time goes in v2:
time: 158 us; the launch traced here: 157 us
  Pallas kernels  150 us (95%)
  local copies, waits for them, and re-layouts  4.45 us (3%)
  other arithmetic  2.18 us (1%)
    pallas_call x1, Pallas kernels, call(): pl.pallas_call(kernel, out_shape=out_shape, in_specs=in_specs, out_specs=...  150 us

profile of v2, /device:TPU:1, one launch (start us, length us, event | category | flops | bytes accessed | tf_op | source)
XLA Modules:
  0.0 157.3 jit_solution(8253728903206400969)
XLA Ops:
  0.6 0.0 copy-start
  0.6 0.0 copy-start.1
  0.7 1.4 pad.4.dec
  2.1 1.5 broadcast_in_dim.8.idx
  3.5 150.0 %whole.1 = (f32[16,16,128]{2,1,0:T(8,128)}, bf16[4,512,128]{2,1,0:T(8,128)(2,1)}) custom-call(bf16[4,512,128]{2,1,0:T(8,128)(2,1)} %state.1, bf16[1024,128]{1,0:T(8,128)(2,1)} %wq.1, bf16[1024,128]{1,0:T(8,128)(2,1)} %wk.1, bf16[1024,128]{1,0:T(8,128)(2,1)} %wv.1, bf16[128,1024]{1,0:T(8,128)(2,1)} %wo.1, bf16[80,128]{1,0:T(8,128)(2,1)} %pad.4.dec, ...), custom_call_target="tpu_custom_call" | custom-call | tf_op jit(solution)/shard_map/whole/pallas_call | solution.py:88
  153.5 0.0 copy-done
  153.5 0.0 copy-done.1
  153.5 2.2 %convert_add_fusion = f32[4,512,128]{2,1,0:T(8,128)} fusion(bf16[4,512,128]{2,1,0:T(8,128)(2,1)} %get-tuple-element.5, bf16[4,512,128]{2,1,0:T(8,128)(2,1)S(1)} %copy-done.1, bf16[4,512,128]{2,1,0:T(8,128)(2,1)S(1)} %copy-done), kind=kLoop, calls=%fused_computation | loop fusion | flops 1310720 | bytes 2621440 | tf_op jit(solution)/shard_map/add | solution.py:668
  155.7 1.6 copy.16
Async XLA Ops:
  0.6 152.9 %copy-start = (bf16[4,512,128]{2,1,0:T(8,128)(2,1)S(1)}, bf16[4,512,128]{2,1,0:T(8,128)(2,1)}, u32[]{:S(2)}) copy-start(bf16[4,512,128]{2,1,0:T(8,128)(2,1)} %state.1) | copy-start | bytes 1572868
  0.6 152.9 %copy-start.1 = (bf16[4,512,128]{2,1,0:T(8,128)(2,1)S(1)}, bf16[4,512,128]{2,1,0:T(8,128)(2,1)}, u32[]{:S(2)}) copy-start(bf16[4,512,128]{2,1,0:T(8,128)(2,1)} %param.13) | copy-start | bytes 1572868

commit v3 on v2

v3 whole, which is shorter than its diff:
```python
import functools

import jax
import jax.numpy as jnp
from jax import lax
from jax.experimental import pallas as pl
from jax.experimental.pallas import tpu as pltpu
from jax.sharding import PartitionSpec as P

D = 1024
HD = 64
VARS = 69
EPSILON = 1e-05
VP = 80
T = 256
G = 8
L = 16
BIG = 1e30
MESH = pl.DeviceIdType.MESH
BF = jnp.bfloat16
F32 = jnp.float32
VMEM_LIMIT = 62 * 1024 * 1024


def nn(a, b):
    return lax.dot_general(a, b, (((1,), (0,)), ((), ())), preferred_element_type=F32)


def nt(a, b):
    return lax.dot_general(a, b, (((1,), (1,)), ((), ())), preferred_element_type=F32)


def place():
    b = lax.axis_index("lat")
    c = lax.axis_index("chan")
    k = b % 2
    big = b // 2
    q = 2 * (c % 4) + k
    row = q + (big % 2) * (7 - 2 * q)
    return b, c, k, big, row, c // 4


def holder(big, row, w):
    q = row + (big % 2) * (7 - 2 * row)
    return big * 2 + q % 2, w * 4 + q // 2


def neighbours():
    b, c, k, big, row, w = place()
    q = 2 * (c % 4) + k
    step = 1 - 2 * (big % 2)
    inner_up = (row > 0).astype(jnp.int32)
    inner_down = (row < 7).astype(jnp.int32)
    q_up, q_down = q - step * inner_up, q + step * inner_down
    up = ((big - 1 + inner_up) * 2 + q_up % 2, w * 4 + q_up // 2)
    down = ((big + 1 - inner_down) * 2 + q_down % 2, w * 4 + q_down // 2)
    return up, down, big * 8 + row > 0, big * 8 + row < 4 * L - 1


def lat_peer(i):
    b, c = lax.axis_index("lat"), lax.axis_index("chan")
    return ((b + i) % L, c)


def far_flip():
    b, c = lax.axis_index("lat"), lax.axis_index("chan")
    return (b + 2 - 4 * ((b // 2) % 2), (c + 4) % G)


def greet():
    b, c, k, big, _, _ = place()
    barrier = pltpu.get_barrier_semaphore()
    peers = [(b, (c + i) % G) for i in range(1, G)]
    peers += [(b + 1 - 2 * k, (c + i) % G) for i in range(G)]
    peers += [(2 * ((big + i) % 8) + j, c) for i in range(1, 8) for j in range(2)]
    peers.append(far_flip())
    for dev in peers:
        pl.semaphore_signal(barrier, inc=1, device_id=dev, device_id_type=MESH)
    pl.semaphore_wait(barrier, len(peers))


def remote(src, dst, ss, rs, dev):
    return pltpu.make_async_remote_copy(
        src_ref=src, dst_ref=dst, send_sem=ss, recv_sem=rs, device_id=dev, device_id_type=MESH
    )


def call(kernel, out_shape, in_specs, out_specs, scratch, cid, name, args):
    return pl.pallas_call(
        kernel,
        out_shape=out_shape,
        in_specs=in_specs,
        out_specs=out_specs,
        scratch_shapes=scratch,
        compiler_params=pltpu.CompilerParams(
            collective_id=cid, has_side_effects=cid is not None, vmem_limit_bytes=VMEM_LIMIT
        ),
        name=name,
    )(*args)


VM = pl.BlockSpec(memory_space=pltpu.VMEM)
ANY = pl.BlockSpec(memory_space=pl.ANY)
DMA = pltpu.SemaphoreType.DMA


def sds(shape, dtype):
    return jax.ShapeDtypeStruct(shape, dtype)


class Spread:
    def __init__(self, view, size, sems):
        self.view, self.half = view, size // 2
        self.s1, self.r1, self.s2, self.r2, self.s3, self.r3, self.s4, self.r4, self.s5, self.r5 = sems
        b, c, k, _, _, z = place()
        x, y = c % 4, b // 4
        p = y % 2
        self.b, self.c, self.x, self.z = b, c, x, z
        self.start = (p * 2 + k) * size
        self.across = ((1 - p) * 2 + k) * size
        self.turn = (1 - 2 * k) * size
        self.core = (b + 1 - 2 * k, c)
        self.ups = [((b + 4) % L, c), ((b + 12) % L, c)]
        self.flips = [(b, (c + 4) % G), far_flip()]
        self.sent = []

    def send(self, g, start, size, ss, rs, dev):
        ref = self.view(g, start, size)
        copy = remote(ref, ref, ss, rs, dev)
        copy.start()
        self.sent.append(copy)

    def wait(self, g, start, size, rs):
        ref = self.view(g, start, size)
        remote(ref, ref, self.s1.at[0], rs, self.core).wait_recv()

    def from_x(self, i):
        return self.z * 4 + (self.x + 4 - i) % 4

    def from_z(self, i):
        return (1 - self.z) * 4 + (self.x + 4 - i) % 4

    def others(self):
        return [self.from_x(i) for i in (1, 3, 2)] + [self.from_z(i) for i in (0, 1, 3, 2)]

    def along_z(self, g):
        for h in range(2):
            at = self.start + h * self.half
            self.send(g, at, self.half, self.s2.at[h, g], self.r2.at[h, g], self.flips[h])

    def first(self):
        for i in (1, 3, 2):
            dev = (self.b, self.z * 4 + (self.x + i) % 4)
            self.send(self.c, self.start, 2 * self.half, self.s1.at[i], self.r1.at[self.c], dev)
        self.along_z(self.c)

    def fan(self, g, h):
        at = self.start + h * self.half
        self.send(g, at, self.half, self.s4.at[h, g], self.r4.at[h, g], self.ups[h])
        self.send(g, at, self.half, self.s3.at[h, g], self.r3.at[h, g], self.core)

    def relay_x(self):
        for i in (1, 3, 2):
            g = self.from_x(i)
            self.wait(g, self.start, 2 * self.half, self.r1.at[g])
            self.along_z(g)
            self.fan(g, 0)
            self.fan(g, 1)

    def relay_z(self):
        for i in (0, 1, 3, 2):
            g = self.from_z(i)
            for h in range(2):
                self.wait(g, self.start + h * self.half, self.half, self.r2.at[h, g])
                self.fan(g, h)

    def relay_y(self):
        for g in self.others():
            for h in range(2):
                at = self.across + h * self.half
                self.wait(g, at, self.half, self.r4.at[h, g])
                self.send(g, at, self.half, self.s5.at[h, g], self.r5.at[h, g], self.core)

    def ready(self):
        for g in self.others():
            for h in range(2):
                self.wait(g, self.start + self.turn + h * self.half, self.half, self.r3.at[h, g])
                self.wait(g, self.across + self.turn + h * self.half, self.half, self.r5.at[h, g])

    def finish(self):
        for copy in self.sent:
            copy.wait_send()


def wide(ref, h):
    return jnp.concatenate([ref[h, g] for g in range(G)], axis=1)


def moments(x):
    mean = jnp.sum(x, axis=-1, keepdims=True) * (1.0 / D)
    centred = x - mean
    var = jnp.sum(centred * centred, axis=-1, keepdims=True) * (1.0 / D)
    inv = lax.rsqrt(var + EPSILON)
    return centred * inv, inv


def only(value, hh):
    first = lax.broadcasted_iota(jnp.int32, value.shape, 1) < HD
    keep = first if hh == 0 else jnp.logical_not(first)
    return jnp.where(keep, value, jnp.zeros_like(value))


def swap_rows(src, above, below, ss, rs):
    up, down, has_up, has_down = neighbours()
    to_up = remote(src, below, ss.at[0], rs.at[0], up)
    to_down = remote(src, above, ss.at[1], rs.at[1], down)

    def start():
        pl.when(has_up)(lambda: to_up.start())
        pl.when(has_down)(lambda: to_down.start())

    def wait():
        @pl.when(has_up)
        def _():
            to_up.wait_send()
            to_down.wait_recv()

        @pl.when(has_down)
        def _():
            to_down.wait_send()
            to_up.wait_recv()

    return start, wait


def loop(n, step):
    def wrapped(i, carry):
        step(i)
        return carry

    lax.fori_loop(0, n, wrapped, 0)


SCRATCH = dict(
    x_v=pltpu.VMEM((3, G, T, 128), BF),
    w_v=pltpu.VMEM((G, 3, D, 128), BF),
    o_v=pltpu.VMEM((G, 128, D), BF),
    d_v=pltpu.VMEM((G, VP, 128), BF),
    i_v=pltpu.VMEM((L, 16, 128), jnp.int32),
    itp=pltpu.VMEM((L, 16, 128, 128), BF),
    n_v=pltpu.VMEM((3 * T, D), BF),
    qkv=pltpu.VMEM((3, G, 3 * T, 128), BF),
    kt=pltpu.VMEM((G, 128, 3 * T), BF),
    mix=pltpu.VMEM((G, T, 128), BF),
    acc=pltpu.VMEM((T, D), F32),
    ml=pltpu.VMEM((2, 16, 1, T), F32),
    mlh=pltpu.VMEM((2, 2, 16, 1, T), F32),
    fields=pltpu.VMEM((G, VP, T), BF),
    mine=pltpu.VMEM((L, 16, 128), BF),
    picked=pltpu.VMEM((L, 16, 128), BF),
    am=pltpu.VMEM((L, 32, 128), BF),
    came=pltpu.VMEM((L, 32, 128), BF),
    parts=pltpu.VMEM((G, VP, T), BF),
    got=pltpu.VMEM((G, VP, T), BF),
    gf=pltpu.VMEM((3, VP, T), F32),
    gu=pltpu.VMEM((T, D), F32),
    low=pltpu.VMEM((3 * T, D), BF),
    do=pltpu.VMEM((G, 3 * T, 128), BF),
    dq=pltpu.VMEM((G, T, 128), BF),
    dkv=pltpu.VMEM((2, G, T, 128), F32),
    delta=pltpu.VMEM((16, 1, T), F32),
    delta_h=pltpu.VMEM((2, 16, 1, T), F32),
    outgo=pltpu.VMEM((G, T, 128), BF),
    f_own=pltpu.VMEM((VP, T), BF),
    i_own=pltpu.VMEM((L, 16, 128), jnp.int32),
    loc=DMA((8,)),
    s_state=DMA((G,)), r_state=DMA((G,)),
    s_d=DMA((G,)), r_d=DMA((G,)),
    s_i=DMA((L,)), r_i=DMA((L,)),
    s_h=DMA((2, G)), r_h=DMA((2, G)),
    s_f=DMA((G,)), r_f=DMA((G,)),
    s_p=DMA((L,)), r_p=DMA((L,)),
    s_a=DMA((L,)), r_a=DMA((L,)),
    s_g=DMA((G,)), r_g=DMA((G,)),
    s_y=DMA((G,)), r_y=DMA((G,)),
    s_m=DMA((2,)), r_m=DMA((2,)),
    s_gh=DMA((2,)), r_gh=DMA((2,)),
    s_dl=DMA((2, 2)), r_dl=DMA((2, 2)),
    w1=DMA((4,)), w2=DMA((G,)), w3=DMA((2, G)), w4=DMA((2, G)), w5=DMA((2, G)), w6=DMA((2, G)), w7=DMA((2, G)), w8=DMA((2, G)), w9=DMA((2, G)), w10=DMA((2, G)),
    o1=DMA((4,)), o2=DMA((G,)), o3=DMA((2, G)), o4=DMA((2, G)), o5=DMA((2, G)), o6=DMA((2, G)), o7=DMA((2, G)), o8=DMA((2, G)), o9=DMA((2, G)), o10=DMA((2, G)),
)


class Refs:
    pass


def kernel(state, wq, wk, wv, wo, dec, idx, gain, interp, obs, count, misfit, back, *scratch):
    s = Refs()
    for name, ref in zip(SCRATCH, scratch):
        setattr(s, name, ref)
    b, c, k, big, row8, w = place()
    r = row8 % 4
    band = 2 * big + row8 // 4
    j_own = r * 2 + w
    home = band == b
    up, down, has_up, has_down = neighbours()
    up_bias = jnp.where(has_up, 0.0, -BIG).astype(F32)
    down_bias = jnp.where(has_down, 0.0, -BIG).astype(F32)
    own_rows = pl.ds(0, T)
    eighth = jnp.asarray(0.125, BF)
    away = jnp.logical_not(home)
    windows = [holder(big, 4 * k + j // 2, j % 2) for j in range(G)]
    mine_at = [jnp.logical_and(home, j_own == j) for j in range(G)]
    members = [(band, (c + i) % G) for i in range(G)]

    local = [
        pltpu.make_async_copy(wq, s.w_v.at[c, 0], s.loc.at[0]),
        pltpu.make_async_copy(wk, s.w_v.at[c, 1], s.loc.at[1]),
        pltpu.make_async_copy(wv, s.w_v.at[c, 2], s.loc.at[2]),
        pltpu.make_async_copy(wo, s.o_v.at[c], s.loc.at[3]),
    ]
    for copy in local:
        copy.start()

    @pl.when(jnp.logical_not(has_up))
    def _():
        s.x_v[0] = jnp.zeros((G, T, 128), BF)

    @pl.when(jnp.logical_not(has_down))
    def _():
        s.x_v[2] = jnp.zeros((G, T, 128), BF)

    s.mlh[:, 0] = jnp.full((2, 16, 1, T), BIG, F32)
    s.mlh[:, 1] = jnp.zeros((2, 16, 1, T), F32)
    s.delta_h[...] = jnp.zeros_like(s.delta_h)
    s.gf[...] = jnp.zeros_like(s.gf)
    eye = lax.broadcasted_iota(jnp.int32, (VP, VARS), 0) == lax.broadcasted_iota(jnp.int32, (VP, VARS), 1)
    s.d_v[c] = nt(eye.astype(F32).astype(BF), dec[...]).astype(BF)
    for n in range(16):
        s.i_own[:, n, :] = jnp.broadcast_to(idx[:, n : n + 1], (L, 128))
    s.i_v[b] = s.i_own[b]
    greet()

    sends = []

    def send_state(j, act):
        src = state.at[j // 2, pl.ds((j % 2) * T, T)]

        @pl.when(jnp.logical_not(mine_at[j]))
        def _():
            copy = remote(src, s.x_v.at[1, c], s.s_state.at[j], s.r_state.at[c], windows[j])
            copy.start() if act else copy.wait_send()

        if act:
            @pl.when(mine_at[j])
            def _():
                pltpu.make_async_copy(src, s.x_v.at[1, c], s.loc.at[4]).start()

    for j in range(G):
        send_state(j, True)
    weights = Spread(
        lambda g, at, n: s.w_v.at[g, :, pl.ds(at, n)], 256, (s.w1, s.w2, s.w3, s.w4, s.w5, s.w6, s.w7, s.w8, s.w9, s.w10)
    )
    outs = Spread(
        lambda g, at, n: s.o_v.at[g, pl.ds(at, n)], 32, (s.o1, s.o2, s.o3, s.o4, s.o5, s.o6, s.o7, s.o8, s.o9, s.o10)
    )
    for copy in local[:3]:
        copy.wait()
    weights.first()
    fetch = pltpu.make_async_copy(interp, s.itp, s.loc.at[5])
    fetch.start()
    for i in range(1, L):
        dev = lat_peer(i)
        copy = remote(s.i_own.at[dev[0]], s.i_v.at[b], s.s_i.at[i], s.r_i.at[i], dev)
        copy.start()
        sends.append(copy)

    def halo(g, sem):
        to_up = remote(s.x_v.at[1, g], s.x_v.at[2, g], s.s_h.at[0, sem], s.r_h.at[0, sem], up)
        to_down = remote(s.x_v.at[1, g], s.x_v.at[0, g], s.s_h.at[1, sem], s.r_h.at[1, sem], down)
        return to_up, to_down

    def start_halo(g, sem):
        to_up, to_down = halo(g, sem)
        pl.when(has_up)(lambda: to_up.start())
        pl.when(has_down)(lambda: to_down.start())

    def got_state(g):
        piece = s.x_v.at[1, g]
        remote(piece, piece, s.s_state.at[0], s.r_state.at[g], members[1]).wait_recv()

    @pl.when(home)
    def _():
        pltpu.make_async_copy(state.at[0, pl.ds(0, T)], s.x_v.at[1, c], s.loc.at[4]).wait()

    pl.when(away)(lambda: got_state(c))
    start_halo(c, 0)
    for i in (1, 3, 4, 5, 7, 2, 6):
        g = (c + i) % G
        got_state(g)
        start_halo(g, i)
    weights.relay_x()
    local[3].wait()
    outs.first()
    for i in range(1, G):
        copy = remote(s.d_v.at[c], s.d_v.at[c], s.s_d.at[i], s.r_d.at[i], (b, (c + i) % G))
        copy.start()
        sends.append(copy)

    def norm(h, at):
        hat, _ = moments(wide(s.x_v, h).astype(F32))
        s.n_v[pl.ds(at * T, T), :] = (hat * gain[...]).astype(BF)

    norm(1, 0)
    weights.relay_z()
    weights.relay_y()

    def project(rows, n):
        def step(m):
            both = [s.w_v[2 * m + e, i] for e in range(2) for i in range(3)]
            res = nn(s.n_v[pl.ds(rows, n), :], jnp.concatenate(both, axis=1))
            for e in range(2):
                for i in range(3):
                    s.qkv[i, 2 * m + e, pl.ds(rows, n), :] = res[:, (3 * e + i) * 128 : (3 * e + i + 1) * 128].astype(BF)

        return step

    weights.ready()
    loop(G // 2, project(0, T))
    for i in range(G):
        to_up, to_down = halo((c + i) % G, i)
        pl.when(has_down)(lambda: to_up.wait_recv())
        pl.when(has_up)(lambda: to_down.wait_recv())
    norm(0, 1)
    norm(2, 2)
    loop(G // 2, project(T, 2 * T))

    def attend(g):
        query = s.qkv[0, g, own_rows, :] * eighth
        s.kt[g] = jnp.transpose(s.qkv[1, g].astype(F32)).astype(BF)
        vt = jnp.transpose(s.qkv[2, g].astype(F32)).astype(BF)
        parts = []
        for hh in range(2):
            q = only(query, hh)
            sc = nt(s.qkv[1, g], q)
            m0 = jnp.max(sc[:T], axis=0, keepdims=True)
            m1 = jnp.max(sc[T : 2 * T], axis=0, keepdims=True) + up_bias
            m2 = jnp.max(sc[2 * T :], axis=0, keepdims=True) + down_bias
            m = jnp.maximum(jnp.maximum(m0, m1), m2)
            e0 = jnp.exp(sc[:T] - m)
            e1 = jnp.exp(sc[T : 2 * T] - (m - up_bias))
            e2 = jnp.exp(sc[2 * T :] - (m - down_bias))
            l = jnp.sum(e0, axis=0, keepdims=True) + jnp.sum(e1, axis=0, keepdims=True) + jnp.sum(e2, axis=0, keepdims=True)
            inv = 1.0 / l
            p = jnp.concatenate([(e0 * inv).astype(BF), (e1 * inv).astype(BF), (e2 * inv).astype(BF)], axis=0)
            parts.append(nn(vt[hh * HD : (hh + 1) * HD], p))
            s.ml[0, 2 * g + hh] = m
            s.ml[1, 2 * g + hh] = inv
        s.mix[g] = jnp.transpose(jnp.concatenate(parts, axis=0)).astype(BF)

    loop(2, attend)
    outs.relay_x()
    loop(2, lambda g: attend(g + 2))
    outs.relay_z()
    loop(2, lambda g: attend(g + 4))
    outs.relay_y()
    loop(2, lambda g: attend(g + 6))
    start_ml, wait_ml = swap_rows(s.ml, s.mlh.at[0], s.mlh.at[1], s.s_m, s.r_m)
    start_ml()
    outs.ready()
    for i in range(1, G):
        remote(s.d_v.at[c], s.d_v.at[c], s.s_d.at[i], s.r_d.at[i], members[i]).wait_recv()
    s.acc[...] = jnp.zeros_like(s.acc)

    def out(g):
        s.acc[...] += nn(s.mix[g], s.o_v[g]).astype(BF).astype(F32)

    loop(G, out)
    updated = (wide(s.x_v, 1).astype(F32) + s.acc[...]).astype(BF)
    dec_all = jnp.concatenate([s.d_v[g] for g in range(G)], axis=1)
    s.f_own[...] = nt(dec_all, updated).astype(BF)

    def send_fields(i, act):
        copy = remote(s.f_own, s.fields.at[j_own], s.s_f.at[i], s.r_f.at[j_own], members[i])
        copy.start() if act else copy.wait_send()

    for i in range(1, G):
        send_fields(i, True)
    pl.when(away)(lambda: send_fields(0, True))

    @pl.when(home)
    def _():
        s.fields[j_own] = s.f_own[...]

    for i in range(1, L):
        remote(s.i_own.at[b], s.i_v.at[b], s.s_i.at[i], s.r_i.at[i], lat_peer(i)).wait_recv()
    index = s.i_v[...].reshape(16 * L, 128)
    lanes = lax.broadcasted_iota(jnp.int32, (16 * L, 128), 1) * 16

    total = jnp.zeros((16 * L, 128), F32)
    for j in range(G):
        @pl.when(jnp.logical_not(mine_at[j]))
        def _():
            remote(s.f_own, s.fields.at[j], s.s_f.at[0], s.r_f.at[j], windows[j]).wait_recv()

        for half in range(2):
            hot = (index == lanes + (2 * j + half)).astype(F32).astype(BF)
            total = total + nn(hot[:, :VP], s.fields[j, :, pl.ds(half * 128, 128)])
    s.mine[...] = total.astype(BF).reshape(L, 16, 128)
    for i in range(1, L):
        dev = lat_peer(i)
        copy = remote(s.mine.at[dev[0]], s.picked.at[b], s.s_p.at[i], s.r_p.at[i], dev)
        copy.start()
        sends.append(copy)
    s.picked[b] = s.mine[b]

    fetch.wait()
    row = lax.broadcasted_iota(jnp.int32, (16, 128), 0)

    def observe(i):
        other_b = (b + L - i) % L

        @pl.when(i > 0)
        def _():
            remote(s.mine.at[b], s.picked.at[b], s.s_p.at[i], s.r_p.at[i], (other_b, c)).wait_recv()

        flat = s.itp[other_b].reshape(2048, 128)
        big = nt(s.picked[other_b], flat)
        pred = jnp.zeros((16, 128), F32)
        for n in range(16):
            pred = jnp.where(row == n, big[:, n * 128 : (n + 1) * 128], pred)
        mis = jnp.where(row < count[other_b], pred - obs[other_b].astype(F32), 0.0).astype(BF)
        lhs = jnp.concatenate([jnp.where(row == n, mis, jnp.zeros_like(mis)) for n in range(16)], axis=1)
        s.am[other_b, :16, :] = nn(lhs, flat).astype(BF)
        s.am[other_b, 16:, :] = mis

        @pl.when(i > 0)
        def _():
            remote(s.am.at[other_b], s.came.at[b], s.s_a.at[i], s.r_a.at[i], (other_b, c)).start()

    loop(L, observe)
    s.came[b] = s.am[b]

    index_t = jnp.transpose(index.astype(F32))[:VP].astype(jnp.int32)
    sub = lax.broadcasted_iota(jnp.int32, (VP, 16 * L), 0) * 16

    def arrived(i):
        other_b = (b + i) % L

        @pl.when(i > 0)
        def _():
            remote(s.am.at[b], s.came.at[b], s.s_a.at[i], s.r_a.at[i], (other_b, c)).wait()

    loop(L, arrived)
    misfit[...] = s.came[:, 16:, :].astype(F32)
    adjoint = s.came[:, :16, :].reshape(16 * L, 128)
    for j in range(G):
        for half in range(2):
            hot = (index_t == sub + (2 * j + half)).astype(F32).astype(BF)
            s.parts[j, :, pl.ds(half * 128, 128)] = nn(hot, adjoint).astype(BF)

        @pl.when(jnp.logical_not(mine_at[j]))
        def _():
            remote(s.parts.at[j], s.got.at[c], s.s_g.at[j], s.r_g.at[c], windows[j]).start()

        @pl.when(mine_at[j])
        def _():
            s.got[c] = s.parts[j]

    def got_part(g):
        remote(s.parts.at[0], s.got.at[g], s.s_g.at[0], s.r_g.at[g], members[1]).wait_recv()

    pl.when(away)(lambda: got_part(c))
    total = s.got[c].astype(F32)
    for i in range(1, G):
        got_part((c + i) % G)
        total = total + s.got[(c + i) % G].astype(F32)
    s.gf[0] = total
    start_gf, wait_gf = swap_rows(s.gf.at[0], s.gf.at[1], s.gf.at[2], s.s_gh, s.r_gh)
    start_gf()
    wait_ml()

    dec_all = jnp.concatenate([dec_all, jnp.zeros((128 - VP, D), BF)], axis=0)
    dec3 = jnp.concatenate([dec_all, dec_all, dec_all], axis=0)

    def update_of(h):
        field = jnp.transpose(jnp.concatenate([s.gf[h], jnp.zeros((128 - VP, T), F32)], axis=0))
        hi = field.astype(BF)
        rest = field - hi.astype(F32)
        mid = rest.astype(BF)
        lo = (rest - mid.astype(F32)).astype(BF)
        update = nn(jnp.concatenate([hi, mid, lo], axis=1), dec3)
        s.low[pl.ds(h * T, T), :] = update.astype(BF)
        return update

    s.gu[...] = update_of(0)
    wait_gf()
    update_of(1)
    update_of(2)

    def mixed(m):
        res = nt(s.low[...], jnp.concatenate([s.o_v[2 * m], s.o_v[2 * m + 1]], axis=0)).astype(BF)
        s.do[2 * m] = res[:, :128]
        s.do[2 * m + 1] = res[:, 128:]

    loop(G // 2, mixed)

    def own(g):
        query = s.qkv[0, g, own_rows, :] * eighth
        parts = []
        dk = jnp.zeros((T, 128), F32)
        dv = jnp.zeros((T, 128), F32)
        for hh in range(2):
            n = 2 * g + hh
            q = only(query, hh)
            d = only(s.do[g, own_rows, :], hh)
            m, inv = s.ml[0, n], s.ml[1, n]
            sc = nt(s.qkv[1, g], q)
            dp = nt(s.qkv[2, g], d)
            p0 = jnp.exp(sc[:T] - m) * inv
            p1 = jnp.exp(sc[T : 2 * T] - (m - up_bias)) * inv
            p2 = jnp.exp(sc[2 * T :] - (m - down_bias)) * inv
            p = jnp.concatenate([p0, p1, p2], axis=0)
            along = jnp.sum(p * dp, axis=0, keepdims=True)
            s.delta[n] = along
            ds = (p * (dp - along)).astype(BF)
            parts.append(nn(s.kt[g, pl.ds(hh * HD, HD), :], ds) * 0.125)
            dk = dk + nn(ds[:T], q)
            dv = dv + nn(p0.astype(BF), d)
        s.dq[g] = jnp.transpose(jnp.concatenate(parts, axis=0)).astype(BF)
        s.dkv[0, g] = dk
        s.dkv[1, g] = dv

    def other(g):
        dk = s.dkv[0, g]
        dv = s.dkv[1, g]
        for side in range(2):
            rows = pl.ds((1 + side) * T, T)
            query = s.qkv[0, g, rows, :] * eighth
            for hh in range(2):
                n = 2 * g + hh
                q = only(query, hh)
                d = only(s.do[g, rows, :], hh)
                sc = nt(s.qkv[1, g, own_rows, :], q)
                dp = nt(s.qkv[2, g, own_rows, :], d)
                p = jnp.exp(sc - s.mlh[side, 0, n]) * s.mlh[side, 1, n]
                ds = (p * (dp - s.delta_h[side, n])).astype(BF)
                dk = dk + nn(ds, q)
                dv = dv + nn(p.astype(BF), d)
        three = jnp.concatenate([s.dq[g], dk.astype(BF), dv.astype(BF)], axis=1)
        wide_w = jnp.concatenate([s.w_v[g, 0], s.w_v[g, 1], s.w_v[g, 2]], axis=1)
        s.acc[...] += nt(three, wide_w).astype(BF).astype(F32)

    swaps = []
    for n in range(2):
        loop(4, lambda g: own(g + 4 * n))
        heads = pl.ds(8 * n, 8)
        start, wait = swap_rows(
            s.delta.at[heads], s.delta_h.at[0, heads], s.delta_h.at[1, heads], s.s_dl.at[n], s.r_dl.at[n]
        )
        start()
        swaps.append(wait)
    s.acc[...] = jnp.zeros_like(s.acc)
    for n in range(2):
        swaps[n]()
        loop(4, lambda g: other(g + 4 * n))

    hat, inv = moments(wide(s.x_v, 1).astype(F32))
    grad_hat = s.acc[...] * gain[...]
    mean = jnp.sum(grad_hat, axis=-1, keepdims=True) * (1.0 / D)
    cross = jnp.sum(grad_hat * hat, axis=-1, keepdims=True) * (1.0 / D)
    total = (s.gu[...] + (grad_hat - mean - hat * cross) * inv).astype(BF)
    for g in range(G):
        s.outgo[g] = total[:, g * 128 : (g + 1) * 128]
    def send_back(i, act):
        dev = members[i]
        copy = remote(s.outgo.at[dev[1]], back.at[r, pl.ds(w * T, T)], s.s_y.at[i], s.r_y.at[j_own], dev)
        copy.start() if act else copy.wait_send()

    for i in range(1, G):
        send_back(i, True)
    pl.when(away)(lambda: send_back(0, True))

    @pl.when(home)
    def _():
        back[r, pl.ds(w * T, T), :] = s.outgo[c]

    weights.finish()
    outs.finish()
    for copy in sends:
        copy.wait_send()
    for i in range(G):
        to_up, to_down = halo((c + i) % G, i)
        pl.when(has_up)(lambda: to_up.wait_send())
        pl.when(has_down)(lambda: to_down.wait_send())
    for i in range(1, G):
        send_fields(i, False)
        send_back(i, False)

    @pl.when(away)
    def _():
        send_fields(0, False)
        send_back(0, False)

    for j in range(G):
        send_state(j, False)

        @pl.when(jnp.logical_not(mine_at[j]))
        def _():
            remote(s.parts.at[j], s.got.at[c], s.s_g.at[j], s.r_g.at[c], windows[j]).wait_send()
            piece = back.at[j // 2, pl.ds((j % 2) * T, T)]
            remote(s.outgo.at[0], piece, s.s_y.at[0], s.r_y.at[j], windows[j]).wait_recv()


def body(state, background, gain, w_query, w_key, w_value, w_out, decoder, interp, obs_values, tile_index, block_count):
    smem = pl.BlockSpec(memory_space=pltpu.SMEM)
    misfit, back = call(
        kernel,
        (sds((L, 16, 128), F32), sds((4, 512, 128), BF)),
        [ANY] * 5 + [VM, VM, VM, ANY, VM, smem],
        [VM] * 2,
        list(SCRATCH.values()),
        0,
        "whole",
        (
            state, w_query, w_key, w_value, w_out, decoder, tile_index.reshape(L, 16), gain.reshape(1, D),
            interp.reshape(L, 16, 128, 128), obs_values.reshape(L, 16, 128), block_count.reshape(L),
        ),
    )
    gradient = state.astype(F32) - background.astype(F32) + back.astype(F32)
    return misfit.reshape(L, 1, 1, 16, 128), gradient


def solution(mesh):
    return jax.shard_map(
        body,
        mesh=mesh,
        in_specs=(
            P("lat", None, "chan"),
            P("lat", None, "chan"),
            P(),
            P(None, "chan"),
            P(None, "chan"),
            P(None, "chan"),
            P("chan", None),
            P("chan", None),
            P("lat", "chan", None, None, None, None),
            P("lat", "chan", None, None, None),
            P("lat", "chan", None, None),
            P("lat", "chan", None),
        ),
        out_specs=(P(None, "chan", "lat", None, None), P("lat", None, "chan")),
        check_vma=False,
    )
```

time: 158 us -> 139 us (0.88)
  Pallas kernels: 150 us -> 133 us
    pallas_call x1, Pallas kernels: 150 us -> 133 us  [call(): pl.pallas_call(kernel, out_shape=out_shape, in_specs=in_specs, out_specs=...]
where the time goes in v3:
time: 139 us
  Pallas kernels  133 us (96%)
  local copies, waits for them, and re-layouts  3.1 us (2%)
  other arithmetic  2.18 us (2%)
    pallas_call x1, Pallas kernels, call(): pl.pallas_call(kernel, out_shape=out_shape, in_specs=in_specs, out_specs=...  133 us
    unnamed x6, local copies, waits for them, and re-layouts  3.1 us

profile of v3, /device:TPU:1, one launch (start us, length us, event | category | flops | bytes accessed | tf_op | source)
XLA Modules:
  0.0 138.8 jit_solution(1226714698977064241)
XLA Ops:
  0.6 0.0 copy-start
  0.6 0.0 copy-start.1
  0.7 1.5 %copy.14.dec = bf16[128,69]{1,0:T(8,128)(2,1)} copy(bf16[128,69]{0,1:T(8,128)(2,1)} %param.19) | data formatting | bytes 35328 | tf_op args[7]
  2.2 132.9 %whole.1 = (f32[16,16,128]{2,1,0:T(8,128)}, bf16[4,512,128]{2,1,0:T(8,128)(2,1)}) custom-call(bf16[4,512,128]{2,1,0:T(8,128)(2,1)} %state.1, bf16[1024,128]{1,0:T(8,128)(2,1)} %wq.1, bf16[1024,128]{1,0:T(8,128)(2,1)} %wk.1, bf16[1024,128]{1,0:T(8,128)(2,1)} %wv.1, bf16[128,1024]{1,0:T(8,128)(2,1)} %wo.1, bf16[128,69]{1,0:T(8,128)(2,1)} %copy.14.dec, ...), custom_call_target="tpu_custom_call" | custom-call | tf_op jit(solution)/shard_map/whole/pallas_call | solution.py:89
  135.1 0.0 copy-done
  135.1 0.0 copy-done.1
  135.1 2.2 %convert_add_fusion = f32[4,512,128]{2,1,0:T(8,128)} fusion(bf16[4,512,128]{2,1,0:T(8,128)(2,1)} %get-tuple-element.5, bf16[4,512,128]{2,1,0:T(8,128)(2,1)S(1)} %copy-done.1, bf16[4,512,128]{2,1,0:T(8,128)(2,1)S(1)} %copy-done), kind=kLoop, calls=%fused_computation | loop fusion | flops 1310720 | bytes 2621440 | tf_op jit(solution)/shard_map/add | solution.py:731
  137.3 1.6 %copy.17 = f32[16,1,1,16,128]{4,3,2,1,0:T(8,128)} copy(f32[16,1,1,16,128]{4,3,2,1,0:T(8,128)} %bitcast.9) | data formatting | bytes 262144
Async XLA Ops:
  0.6 134.4 %copy-start = (bf16[4,512,128]{2,1,0:T(8,128)(2,1)S(1)}, bf16[4,512,128]{2,1,0:T(8,128)(2,1)}, u32[]{:S(2)}) copy-start(bf16[4,512,128]{2,1,0:T(8,128)(2,1)} %state.1) | copy-start | bytes 1572868
  0.6 134.4 %copy-start.1 = (bf16[4,512,128]{2,1,0:T(8,128)(2,1)S(1)}, bf16[4,512,128]{2,1,0:T(8,128)(2,1)}, u32[]{:S(2)}) copy-start(bf16[4,512,128]{2,1,0:T(8,128)(2,1)} %param.13) | copy-start | bytes 1572868

commit v4 on v3

--- a/solution.py
+++ b/solution.py
@@ -122,13 +122,11 @@
         self.core = (b + 1 - 2 * k, c)
         self.ups = [((b + 4) % L, c), ((b + 12) % L, c)]
         self.flips = [(b, (c + 4) % G), far_flip()]
-        self.sent = []
 
     def send(self, g, start, size, ss, rs, dev):
         ref = self.view(g, start, size)
         copy = remote(ref, ref, ss, rs, dev)
         copy.start()
-        self.sent.append(copy)
 
     def wait(self, g, start, size, rs):
         ref = self.view(g, start, size)
@@ -139,9 +137,6 @@
 
     def from_z(self, i):
         return (1 - self.z) * 4 + (self.x + 4 - i) % 4
-
-    def others(self):
-        return [self.from_x(i) for i in (1, 3, 2)] + [self.from_z(i) for i in (0, 1, 3, 2)]
 
     def along_z(self, g):
         for h in range(2):
@@ -159,37 +154,47 @@
         self.send(g, at, self.half, self.s4.at[h, g], self.r4.at[h, g], self.ups[h])
         self.send(g, at, self.half, self.s3.at[h, g], self.r3.at[h, g], self.core)
 
-    def relay_x(self):
+    def relay_x(self, i):
+        g = self.from_x(i)
+        self.wait(g, self.start, 2 * self.half, self.r1.at[g])
+        self.along_z(g)
+        self.fan(g, 0)
+        self.fan(g, 1)
+
+    def relay_z(self, i):
+        g = self.from_z(i)
+        for h in range(2):
+            self.wait(g, self.start + h * self.half, self.half, self.r2.at[h, g])
+            self.fan(g, h)
+
+    def relay_y(self, g):
+        for h in range(2):
+            at = self.across + h * self.half
+            self.wait(g, at, self.half, self.r4.at[h, g])
+            self.send(g, at, self.half, self.s5.at[h, g], self.r5.at[h, g], self.core)
+
+    def ready(self, g):
+        for h in range(2):
+            self.wait(g, self.start + self.turn + h * self.half, self.half, self.r3.at[h, g])
+            self.wait(g, self.across + self.turn + h * self.half, self.half, self.r5.at[h, g])
+
+    def finish(self):
+        def sent(g, start, size, sem):
+            ref = self.view(g, start, size)
+            remote(ref, ref, sem, self.r1.at[0], self.core).wait_send()
+
+        half = self.half
         for i in (1, 3, 2):
-            g = self.from_x(i)
-            self.wait(g, self.start, 2 * self.half, self.r1.at[g])
-            self.along_z(g)
-            self.fan(g, 0)
-            self.fan(g, 1)
-
-    def relay_z(self):
-        for i in (0, 1, 3, 2):
-            g = self.from_z(i)
+            sent(self.c, self.start, 2 * half, self.s1.at[i])
+        for i in range(4):
+            row = self.from_x(i)
             for h in range(2):
-                self.wait(g, self.start + h * self.half, self.half, self.r2.at[h, g])
-                self.fan(g, h)
-
-    def relay_y(self):
-        for g in self.others():
-            for h in range(2):
-                at = self.across + h * self.half
-                self.wait(g, at, self.half, self.r4.at[h, g])
-                self.send(g, at, self.half, self.s5.at[h, g], self.r5.at[h, g], self.core)
-
-    def ready(self):
-        for g in self.others():
-            for h in range(2):
-                self.wait(g, self.start + self.turn + h * self.half, self.half, self.r3.at[h, g])
-                self.wait(g, self.across + self.turn + h * self.half, self.half, self.r5.at[h, g])
-
-    def finish(self):
-        for copy in self.sent:
-            copy.wait_send()
+                at = self.start + h * half
+                sent(row, at, half, self.s2.at[h, row])
+                for g in ([row] if i else []) + [self.from_z(i)]:
+                    sent(g, at, half, self.s3.at[h, g])
+                    sent(g, at, half, self.s4.at[h, g])
+                    sent(g, self.across + h * half, half, self.s5.at[h, g])
 
 
 def wide(ref, h):
@@ -264,13 +269,13 @@
     got=pltpu.VMEM((G, VP, T), BF),
     gf=pltpu.VMEM((3, VP, T), F32),
     gu=pltpu.VMEM((T, D), F32),
-    low=pltpu.VMEM((3 * T, D), BF),
     do=pltpu.VMEM((G, 3 * T, 128), BF),
     dq=pltpu.VMEM((G, T, 128), BF),
-    dkv=pltpu.VMEM((2, G, T, 128), F32),
+    dso=pltpu.VMEM((G, T, 2 * T), BF),
+    p_own=pltpu.VMEM((16, 3 * T, T), F32),
+    p_nb=pltpu.VMEM((2, 16, T, T), F32),
     delta=pltpu.VMEM((16, 1, T), F32),
     delta_h=pltpu.VMEM((2, 16, 1, T), F32),
-    outgo=pltpu.VMEM((G, T, 128), BF),
     f_own=pltpu.VMEM((VP, T), BF),
     i_own=pltpu.VMEM((L, 16, 128), jnp.int32),
     loc=DMA((8,)),
@@ -400,7 +405,9 @@
         g = (c + i) % G
         got_state(g)
         start_halo(g, i)
-    weights.relay_x()
+    weights.relay_z(0)
+    for i in (1, 3, 2):
+        weights.relay_x(i)
     local[3].wait()
     outs.first()
     for i in range(1, G):
@@ -413,37 +420,70 @@
         s.n_v[pl.ds(at * T, T), :] = (hat * gain[...]).astype(BF)
 
     norm(1, 0)
-    weights.relay_z()
-    weights.relay_y()
-
-    def project(rows, n):
-        def step(m):
-            both = [s.w_v[2 * m + e, i] for e in range(2) for i in range(3)]
-            res = nn(s.n_v[pl.ds(rows, n), :], jnp.concatenate(both, axis=1))
-            for e in range(2):
-                for i in range(3):
-                    s.qkv[i, 2 * m + e, pl.ds(rows, n), :] = res[:, (3 * e + i) * 128 : (3 * e + i + 1) * 128].astype(BF)
-
-        return step
-
-    weights.ready()
-    loop(G // 2, project(0, T))
+    weights.relay_y(weights.from_z(0))
+    weights.relay_y(weights.from_x(1))
+    weights.relay_y(weights.from_x(3))
     for i in range(G):
         to_up, to_down = halo((c + i) % G, i)
         pl.when(has_down)(lambda: to_up.wait_recv())
         pl.when(has_up)(lambda: to_down.wait_recv())
     norm(0, 1)
     norm(2, 2)
-    loop(G // 2, project(T, 2 * T))
-
-    def attend(g):
+    weights.relay_z(1)
+    weights.relay_y(weights.from_x(2))
+    weights.relay_z(3)
+
+    def attend(i):
+        t = (i + 1) % 3
+        late = (i >= 2).astype(jnp.int32)
+        over = (i >= 5).astype(jnp.int32) + (i == 1).astype(jnp.int32)
+        back_by = late * (1 + t * (7 - 3 * t) // 2)
+        g = (w + over * (1 - 2 * w)) * 4 + (c % 4 + 4 - back_by) % 4
+
+        def relays(n):
+            return pl.when(i == n)
+
+        pl.when(i > 0)(lambda: weights.ready(g))
+
+        @relays(1)
+        def _():
+            weights.relay_z(2)
+            weights.relay_y(weights.from_z(1))
+
+        @relays(2)
+        def _():
+            weights.relay_y(weights.from_z(3))
+
+        @relays(3)
+        def _():
+            weights.relay_y(weights.from_z(2))
+            outs.relay_z(0)
+            for n in (1, 3, 2):
+                outs.relay_x(n)
+
+        @relays(5)
+        def _():
+            for n in (1, 3, 2):
+                outs.relay_z(n)
+            outs.relay_y(outs.from_z(0))
+            for n in (1, 3, 2):
+                outs.relay_y(outs.from_x(n))
+
+        @relays(7)
+        def _():
+            for n in (1, 3, 2):
+                outs.relay_y(outs.from_z(n))
+
+        res = nn(s.n_v[...], jnp.concatenate([s.w_v[g, n] for n in range(3)], axis=1))
+        for n in range(3):
+            s.qkv[n, g] = res[:, n * 128 : (n + 1) * 128].astype(BF)
+        vt = jnp.transpose(res[:, 256:]).astype(BF)
         query = s.qkv[0, g, own_rows, :] * eighth
-        s.kt[g] = jnp.transpose(s.qkv[1, g].astype(F32)).astype(BF)
-        vt = jnp.transpose(s.qkv[2, g].astype(F32)).astype(BF)
+        scores = [nt(s.qkv[1, g], only(query, hh)) for hh in range(2)]
         parts = []
         for hh in range(2):
-            q = only(query, hh)
-            sc = nt(s.qkv[1, g], q)
+            n = 2 * g + hh
+            sc = scores[hh]
             m0 = jnp.max(sc[:T], axis=0, keepdims=True)
             m1 = jnp.max(sc[T : 2 * T], axis=0, keepdims=True) + up_bias
             m2 = jnp.max(sc[2 * T :], axis=0, keepdims=True) + down_bias
@@ -453,22 +493,22 @@
             e2 = jnp.exp(sc[2 * T :] - (m - down_bias))
             l = jnp.sum(e0, axis=0, keepdims=True) + jnp.sum(e1, axis=0, keepdims=True) + jnp.sum(e2, axis=0, keepdims=True)
             inv = 1.0 / l
-            p = jnp.concatenate([(e0 * inv).astype(BF), (e1 * inv).astype(BF), (e2 * inv).astype(BF)], axis=0)
+            s.p_own[n, :T, :] = e0 * inv
+            s.p_own[n, T : 2 * T, :] = e1 * inv
+            s.p_own[n, 2 * T :, :] = e2 * inv
+            p = s.p_own[n].astype(BF)
             parts.append(nn(vt[hh * HD : (hh + 1) * HD], p))
-            s.ml[0, 2 * g + hh] = m
-            s.ml[1, 2 * g + hh] = inv
+            s.ml[0, n] = m
+            s.ml[1, n] = inv
         s.mix[g] = jnp.transpose(jnp.concatenate(parts, axis=0)).astype(BF)
 
-    loop(2, attend)
-    outs.relay_x()
-    loop(2, lambda g: attend(g + 2))
-    outs.relay_z()
-    loop(2, lambda g: attend(g + 4))
-    outs.relay_y()
-    loop(2, lambda g: attend(g + 6))
+    loop(G, attend)
     start_ml, wait_ml = swap_rows(s.ml, s.mlh.at[0], s.mlh.at[1], s.s_m, s.r_m)
     start_ml()
-    outs.ready()
+    for n in range(4):
+        if n:
+            outs.ready(outs.from_x(n))
+        outs.ready(outs.from_z(n))
     for i in range(1, G):
         remote(s.d_v.at[c], s.d_v.at[c], s.s_d.at[i], s.r_d.at[i], members[i]).wait_recv()
     s.acc[...] = jnp.zeros_like(s.acc)
@@ -515,6 +555,19 @@
         sends.append(copy)
     s.picked[b] = s.mine[b]
 
+    wait_ml()
+
+    def near(g):
+        s.kt[g] = jnp.transpose(s.qkv[1, g].astype(F32)).astype(BF)
+        for side in range(2):
+            query = s.qkv[0, g, pl.ds((1 + side) * T, T), :] * eighth
+            for hh in range(2):
+                n = 2 * g + hh
+                sc = nt(s.qkv[1, g, own_rows, :], only(query, hh))
+                s.p_nb[side, n] = jnp.exp(sc - s.mlh[side, 0, n]) * s.mlh[side, 1, n]
+
+    loop(4, near)
+
     fetch.wait()
     row = lax.broadcasted_iota(jnp.int32, (16, 128), 0)
 
@@ -542,6 +595,8 @@
     loop(L, observe)
     s.came[b] = s.am[b]
 
+    loop(4, lambda g: near(g + 4))
+
     index_t = jnp.transpose(index.astype(F32))[:VP].astype(jnp.int32)
     sub = lax.broadcasted_iota(jnp.int32, (VP, 16 * L), 0) * 16
 
@@ -579,7 +634,6 @@
     s.gf[0] = total
     start_gf, wait_gf = swap_rows(s.gf.at[0], s.gf.at[1], s.gf.at[2], s.s_gh, s.r_gh)
     start_gf()
-    wait_ml()
 
     dec_all = jnp.concatenate([dec_all, jnp.zeros((128 - VP, D), BF)], axis=0)
     dec3 = jnp.concatenate([dec_all, dec_all, dec_all], axis=0)
@@ -591,67 +645,55 @@
         mid = rest.astype(BF)
         lo = (rest - mid.astype(F32)).astype(BF)
         update = nn(jnp.concatenate([hi, mid, lo], axis=1), dec3)
-        s.low[pl.ds(h * T, T), :] = update.astype(BF)
+        s.n_v[pl.ds(h * T, T), :] = update.astype(BF)
         return update
 
-    s.gu[...] = update_of(0)
-    wait_gf()
-    update_of(1)
-    update_of(2)
-
-    def mixed(m):
-        res = nt(s.low[...], jnp.concatenate([s.o_v[2 * m], s.o_v[2 * m + 1]], axis=0)).astype(BF)
-        s.do[2 * m] = res[:, :128]
-        s.do[2 * m + 1] = res[:, 128:]
-
-    loop(G // 2, mixed)
+    def mixed(rows, n):
+        def step(m):
+            weight = jnp.concatenate([s.o_v[2 * m], s.o_v[2 * m + 1]], axis=0)
+            res = nt(s.n_v[pl.ds(rows, n), :], weight).astype(BF)
+            s.do[2 * m, pl.ds(rows, n), :] = res[:, :128]
+            s.do[2 * m + 1, pl.ds(rows, n), :] = res[:, 128:]
+
+        return step
 
     def own(g):
-        query = s.qkv[0, g, own_rows, :] * eighth
         parts = []
-        dk = jnp.zeros((T, 128), F32)
-        dv = jnp.zeros((T, 128), F32)
         for hh in range(2):
             n = 2 * g + hh
-            q = only(query, hh)
-            d = only(s.do[g, own_rows, :], hh)
-            m, inv = s.ml[0, n], s.ml[1, n]
-            sc = nt(s.qkv[1, g], q)
-            dp = nt(s.qkv[2, g], d)
-            p0 = jnp.exp(sc[:T] - m) * inv
-            p1 = jnp.exp(sc[T : 2 * T] - (m - up_bias)) * inv
-            p2 = jnp.exp(sc[2 * T :] - (m - down_bias)) * inv
-            p = jnp.concatenate([p0, p1, p2], axis=0)
+            dp = nt(s.qkv[2, g], only(s.do[g, own_rows, :], hh))
+            p = s.p_own[n]
             along = jnp.sum(p * dp, axis=0, keepdims=True)
             s.delta[n] = along
             ds = (p * (dp - along)).astype(BF)
             parts.append(nn(s.kt[g, pl.ds(hh * HD, HD), :], ds) * 0.125)
-            dk = dk + nn(ds[:T], q)
-            dv = dv + nn(p0.astype(BF), d)
+            s.dso[g, :, pl.ds(hh * T, T)] = ds[:T]
         s.dq[g] = jnp.transpose(jnp.concatenate(parts, axis=0)).astype(BF)
-        s.dkv[0, g] = dk
-        s.dkv[1, g] = dv
 
     def other(g):
-        dk = s.dkv[0, g]
-        dv = s.dkv[1, g]
+        scores, probs, queries, grads = [s.dso[g]], [], [], []
+        for hh in range(2):
+            probs.append(s.p_own[2 * g + hh, :T, :].astype(BF))
+            queries.append(only(s.qkv[0, g, own_rows, :] * eighth, hh))
+            grads.append(only(s.do[g, own_rows, :], hh))
         for side in range(2):
             rows = pl.ds((1 + side) * T, T)
-            query = s.qkv[0, g, rows, :] * eighth
             for hh in range(2):
                 n = 2 * g + hh
-                q = only(query, hh)
-                d = only(s.do[g, rows, :], hh)
-                sc = nt(s.qkv[1, g, own_rows, :], q)
-                dp = nt(s.qkv[2, g, own_rows, :], d)
-                p = jnp.exp(sc - s.mlh[side, 0, n]) * s.mlh[side, 1, n]
-                ds = (p * (dp - s.delta_h[side, n])).astype(BF)
-                dk = dk + nn(ds, q)
-                dv = dv + nn(p.astype(BF), d)
+                queries.append(only(s.qkv[0, g, rows, :] * eighth, hh))
+                grads.append(only(s.do[g, rows, :], hh))
+                dp = nt(s.qkv[2, g, own_rows, :], grads[-1])
+                p = s.p_nb[side, n]
+                scores.append((p * (dp - s.delta_h[side, n])).astype(BF))
+                probs.append(p.astype(BF))
+        dk = nn(jnp.concatenate(scores, axis=1), jnp.concatenate(queries, axis=0))
+        dv = nn(jnp.concatenate(probs, axis=1), jnp.concatenate(grads, axis=0))
         three = jnp.concatenate([s.dq[g], dk.astype(BF), dv.astype(BF)], axis=1)
         wide_w = jnp.concatenate([s.w_v[g, 0], s.w_v[g, 1], s.w_v[g, 2]], axis=1)
         s.acc[...] += nt(three, wide_w).astype(BF).astype(F32)
 
+    s.gu[...] = update_of(0)
+    loop(G // 2, mixed(0, T))
     swaps = []
     for n in range(2):
         loop(4, lambda g: own(g + 4 * n))
@@ -661,6 +703,10 @@
         )
         start()
         swaps.append(wait)
+    wait_gf()
+    update_of(1)
+    update_of(2)
+    loop(G // 2, mixed(T, 2 * T))
     s.acc[...] = jnp.zeros_like(s.acc)
     for n in range(2):
         swaps[n]()
@@ -672,10 +718,10 @@
     cross = jnp.sum(grad_hat * hat, axis=-1, keepdims=True) * (1.0 / D)
     total = (s.gu[...] + (grad_hat - mean - hat * cross) * inv).astype(BF)
     for g in range(G):
-        s.outgo[g] = total[:, g * 128 : (g + 1) * 128]
+        s.mix[g] = total[:, g * 128 : (g + 1) * 128]
     def send_back(i, act):
         dev = members[i]
-        copy = remote(s.outgo.at[dev[1]], back.at[r, pl.ds(w * T, T)], s.s_y.at[i], s.r_y.at[j_own], dev)
+        copy = remote(s.mix.at[dev[1]], back.at[r, pl.ds(w * T, T)], s.s_y.at[i], s.r_y.at[j_own], dev)
         copy.start() if act else copy.wait_send()
 
     for i in range(1, G):
@@ -684,7 +730,7 @@
 
     @pl.when(home)
     def _():
-        back[r, pl.ds(w * T, T), :] = s.outgo[c]
+        back[r, pl.ds(w * T, T), :] = s.mix[c]
 
     weights.finish()
     outs.finish()
@@ -710,7 +756,7 @@
         def _():
             remote(s.parts.at[j], s.got.at[c], s.s_g.at[j], s.r_g.at[c], windows[j]).wait_send()
             piece = back.at[j // 2, pl.ds((j % 2) * T, T)]
-            remote(s.outgo.at[0], piece, s.s_y.at[0], s.r_y.at[j], windows[j]).wait_recv()
+            remote(s.mix.at[0], piece, s.s_y.at[0], s.r_y.at[j], windows[j]).wait_recv()
 
 
 def body(state, background, gain, w_query, w_key, w_value, w_out, decoder, interp, obs_values, tile_index, block_count):

time: 139 us -> 126 us (0.906)
  Pallas kernels: 133 us -> 120 us
    pallas_call x1, Pallas kernels: 133 us -> 120 us  [call(): pl.pallas_call(kernel, out_shape=out_shape, in_specs=in_specs, out_specs=...]
where the time goes in v4:
time: 126 us
  Pallas kernels  120 us (95%)
  local copies, waits for them, and re-layouts  3.1 us (2%)
  other arithmetic  2.18 us (2%)
    pallas_call x1, Pallas kernels, call(): pl.pallas_call(kernel, out_shape=out_shape, in_specs=in_specs, out_specs=...  120 us
    unnamed x6, local copies, waits for them, and re-layouts  3.1 us

profile of v4, /device:TPU:1, one launch (start us, length us, event | category | flops | bytes accessed | tf_op | source)
XLA Modules:
  0.0 126.0 jit_solution(2704966226187325801)
XLA Ops:
  0.6 0.0 copy-start
  0.6 0.0 copy-start.1
  0.7 1.5 %copy.14.dec = bf16[128,69]{1,0:T(8,128)(2,1)} copy(bf16[128,69]{0,1:T(8,128)(2,1)} %param.19) | data formatting | bytes 35328 | tf_op args[7]
  2.2 120.1 %whole.1 = (f32[16,16,128]{2,1,0:T(8,128)}, bf16[4,512,128]{2,1,0:T(8,128)(2,1)}) custom-call(bf16[4,512,128]{2,1,0:T(8,128)(2,1)} %state.1, bf16[1024,128]{1,0:T(8,128)(2,1)} %wq.1, bf16[1024,128]{1,0:T(8,128)(2,1)} %wk.1, bf16[1024,128]{1,0:T(8,128)(2,1)} %wv.1, bf16[128,1024]{1,0:T(8,128)(2,1)} %wo.1, bf16[128,69]{1,0:T(8,128)(2,1)} %copy.14.dec, ...), custom_call_target="tpu_custom_call" | custom-call | tf_op jit(solution)/shard_map/whole/pallas_call | solution.py:89
  122.3 0.0 copy-done
  122.3 0.0 copy-done.1
  122.3 2.2 %convert_add_fusion = f32[4,512,128]{2,1,0:T(8,128)} fusion(bf16[4,512,128]{2,1,0:T(8,128)(2,1)} %get-tuple-element.5, bf16[4,512,128]{2,1,0:T(8,128)(2,1)S(1)} %copy-done.1, bf16[4,512,128]{2,1,0:T(8,128)(2,1)S(1)} %copy-done), kind=kLoop, calls=%fused_computation | loop fusion | flops 1310720 | bytes 2621440 | tf_op jit(solution)/shard_map/add | solution.py:777
  124.5 1.6 %copy.17 = f32[16,1,1,16,128]{4,3,2,1,0:T(8,128)} copy(f32[16,1,1,16,128]{4,3,2,1,0:T(8,128)} %bitcast.9) | data formatting | bytes 262144
Async XLA Ops:
  0.6 121.6 %copy-start = (bf16[4,512,128]{2,1,0:T(8,128)(2,1)S(1)}, bf16[4,512,128]{2,1,0:T(8,128)(2,1)}, u32[]{:S(2)}) copy-start(bf16[4,512,128]{2,1,0:T(8,128)(2,1)} %state.1) | copy-start | bytes 1572868
  0.6 121.6 %copy-start.1 = (bf16[4,512,128]{2,1,0:T(8,128)(2,1)S(1)}, bf16[4,512,128]{2,1,0:T(8,128)(2,1)}, u32[]{:S(2)}) copy-start(bf16[4,512,128]{2,1,0:T(8,128)(2,1)} %param.13) | copy-start | bytes 1572868

commit v5 on v4

--- a/solution.py
+++ b/solution.py
@@ -67,7 +67,7 @@
     return (b + 2 - 4 * ((b // 2) % 2), (c + 4) % G)
 
 
-def greet():
+def greeted():
     b, c, k, big, _, _ = place()
     barrier = pltpu.get_barrier_semaphore()
     peers = [(b, (c + i) % G) for i in range(1, G)]
@@ -76,7 +76,7 @@
     peers.append(far_flip())
     for dev in peers:
         pl.semaphore_signal(barrier, inc=1, device_id=dev, device_id_type=MESH)
-    pl.semaphore_wait(barrier, len(peers))
+    return lambda: pl.semaphore_wait(barrier, len(peers))
 
 
 def remote(src, dst, ss, rs, dev):
@@ -272,6 +272,8 @@
     do=pltpu.VMEM((G, 3 * T, 128), BF),
     dq=pltpu.VMEM((G, T, 128), BF),
     dso=pltpu.VMEM((G, T, 2 * T), BF),
+    dp=pltpu.VMEM((2, 3 * T, T), F32),
+    ds=pltpu.VMEM((2, 3 * T, T), BF),
     p_own=pltpu.VMEM((16, 3 * T, T), F32),
     p_nb=pltpu.VMEM((2, 16, T, T), F32),
     delta=pltpu.VMEM((16, 1, T), F32),
@@ -319,6 +321,7 @@
     mine_at = [jnp.logical_and(home, j_own == j) for j in range(G)]
     members = [(band, (c + i) % G) for i in range(G)]
 
+    met = greeted()
     local = [
         pltpu.make_async_copy(wq, s.w_v.at[c, 0], s.loc.at[0]),
         pltpu.make_async_copy(wk, s.w_v.at[c, 1], s.loc.at[1]),
@@ -341,11 +344,11 @@
     s.delta_h[...] = jnp.zeros_like(s.delta_h)
     s.gf[...] = jnp.zeros_like(s.gf)
     eye = lax.broadcasted_iota(jnp.int32, (VP, VARS), 0) == lax.broadcasted_iota(jnp.int32, (VP, VARS), 1)
-    s.d_v[c] = nt(eye.astype(F32).astype(BF), dec[...]).astype(BF)
+    s.d_v[c] = nn(eye.astype(F32).astype(BF), dec[...]).astype(BF)
     for n in range(16):
         s.i_own[:, n, :] = jnp.broadcast_to(idx[:, n : n + 1], (L, 128))
     s.i_v[b] = s.i_own[b]
-    greet()
+    met()
 
     sends = []
 
@@ -608,7 +611,7 @@
             remote(s.am.at[b], s.came.at[b], s.s_a.at[i], s.r_a.at[i], (other_b, c)).wait()
 
     loop(L, arrived)
-    misfit[...] = s.came[:, 16:, :].astype(F32)
+    misfit[...] = s.came[:, 16:, :]
     adjoint = s.came[:, :16, :].reshape(16 * L, 128)
     for j in range(G):
         for half in range(2):
@@ -658,16 +661,22 @@
         return step
 
     def own(g):
+        for hh in range(2):
+            s.dp[hh] = nt(s.qkv[2, g], only(s.do[g, own_rows, :], hh))
         parts = []
         for hh in range(2):
             n = 2 * g + hh
-            dp = nt(s.qkv[2, g], only(s.do[g, own_rows, :], hh))
-            p = s.p_own[n]
-            along = jnp.sum(p * dp, axis=0, keepdims=True)
+            along = jnp.zeros((8, T), F32)
+            for at in range(0, 3 * T, 64):
+                product = s.p_own[n, at : at + 64, :] * s.dp[hh, at : at + 64, :]
+                along = along + jnp.sum(product.reshape(8, 8, T), axis=0)
+            along = jnp.sum(along, axis=0, keepdims=True)
             s.delta[n] = along
-            ds = (p * (dp - along)).astype(BF)
-            parts.append(nn(s.kt[g, pl.ds(hh * HD, HD), :], ds) * 0.125)
-            s.dso[g, :, pl.ds(hh * T, T)] = ds[:T]
+            for at in range(0, 3 * T, 64):
+                spread = s.p_own[n, at : at + 64, :] * (s.dp[hh, at : at + 64, :] - along)
+                s.ds[hh, at : at + 64, :] = spread.astype(BF)
+            parts.append(nn(s.kt[g, pl.ds(hh * HD, HD), :], s.ds[hh]) * 0.125)
+            s.dso[g, :, pl.ds(hh * T, T)] = s.ds[hh, :T, :]
         s.dq[g] = jnp.transpose(jnp.concatenate(parts, axis=0)).astype(BF)
 
     def other(g):
@@ -759,22 +768,36 @@
             remote(s.mix.at[0], piece, s.s_y.at[0], s.r_y.at[j], windows[j]).wait_recv()
 
 
+def finish_kernel(low, back, state, background, misfit, gradient):
+    misfit[...] = low[...].astype(F32)
+    gradient[...] = state[...].astype(F32) - background[...].astype(F32) + back[...].astype(F32)
+
+
 def body(state, background, gain, w_query, w_key, w_value, w_out, decoder, interp, obs_values, tile_index, block_count):
     smem = pl.BlockSpec(memory_space=pltpu.SMEM)
     misfit, back = call(
         kernel,
-        (sds((L, 16, 128), F32), sds((4, 512, 128), BF)),
+        (sds((L, 16, 128), BF), sds((4, 512, 128), BF)),
         [ANY] * 5 + [VM, VM, VM, ANY, VM, smem],
         [VM] * 2,
         list(SCRATCH.values()),
         0,
         "whole",
         (
-            state, w_query, w_key, w_value, w_out, decoder, tile_index.reshape(L, 16), gain.reshape(1, D),
+            state, w_query, w_key, w_value, w_out, jnp.transpose(decoder), tile_index.reshape(L, 16), gain.reshape(1, D),
             interp.reshape(L, 16, 128, 128), obs_values.reshape(L, 16, 128), block_count.reshape(L),
         ),
     )
-    gradient = state.astype(F32) - background.astype(F32) + back.astype(F32)
+    row = pl.BlockSpec((2, 512, 128), lambda i: (i, 0, 0))
+    part = pl.BlockSpec((8, 16, 128), lambda i: (i, 0, 0))
+    misfit, gradient = pl.pallas_call(
+        finish_kernel,
+        grid=(2,),
+        out_shape=(sds((L, 16, 128), F32), sds((4, 512, 128), F32)),
+        in_specs=[part, row, row, row],
+        out_specs=(part, row),
+        name="finish",
+    )(misfit, back, state, background)
     return misfit.reshape(L, 1, 1, 16, 128), gradient
 
 

time: 126 us -> 120 us (0.952)
  local copies, waits for them, and re-layouts: 3.1 us -> 0 us
  other arithmetic: 2.18 us -> 0 us
    pallas_call x1, Pallas kernels: 120 us -> 117 us  [call(): pl.pallas_call(kernel, out_shape=out_shape, in_specs=in_specs, out_specs=...]
    unnamed x6 -> x0, local copies, waits for them, and re-layouts: 3.1 us -> none
    pallas_call x0 -> x1, Pallas kernels: none -> 2.29 us  [body(): pl.pallas_call(finish_kernel, grid=(2,), out_shape=(sds((L, 16, 128), F32...]
    add x1 -> x0, other arithmetic: 2.18 us -> none  [body(): gradient = state.astype(F32) - background.astype(F32) + back.astype(F32)]
where the time goes in v5:
time: 120 us
  Pallas kernels  119 us (99%)
    pallas_call x1, Pallas kernels, call(): pl.pallas_call(kernel, out_shape=out_shape, in_specs=in_specs, out_specs=...  117 us

profile of v5, /device:TPU:1, one launch (start us, length us, event | category | flops | bytes accessed | tf_op | source)
XLA Modules:
  0.0 119.7 jit_solution(1896355556873887170)
XLA Ops:
  0.6 116.8 %whole.1 = (bf16[16,16,128]{2,1,0:T(8,128)(2,1)}, bf16[4,512,128]{2,1,0:T(8,128)(2,1)}) custom-call(bf16[4,512,128]{2,1,0:T(8,128)(2,1)} %state.3, bf16[1024,128]{1,0:T(8,128)(2,1)} %wq.1, bf16[1024,128]{1,0:T(8,128)(2,1)} %wk.1, bf16[1024,128]{1,0:T(8,128)(2,1)} %wv.1, bf16[128,1024]{1,0:T(8,128)(2,1)} %wo.1, bf16[69,128]{1,0:T(8,128)(2,1)} %bitcast.11, ...), custom_call_target="tpu_custom_call" | custom-call | tf_op jit(solution)/shard_map/whole/pallas_call | solution.py:89
  117.4 2.3 %finish.1 = (f32[16,16,128]{2,1,0:T(8,128)}, f32[4,512,128]{2,1,0:T(8,128)}) custom-call(bf16[16,16,128]{2,1,0:T(8,128)(2,1)} %get-tuple-element.6.low, bf16[4,512,128]{2,1,0:T(8,128)(2,1)} %get-tuple-element.7.back, bf16[4,512,128]{2,1,0:T(8,128)(2,1)} %state.3, bf16[4,512,128]{2,1,0:T(8,128)(2,1)} %background.1), custom_call_target="tpu_custom_call" | custom-call | tf_op jit(solution)/shard_map/finish/pallas_call | solution.py:793

commit v6 on v5

--- a/solution.py
+++ b/solution.py
@@ -274,6 +274,8 @@
     dso=pltpu.VMEM((G, T, 2 * T), BF),
     dp=pltpu.VMEM((2, 3 * T, T), F32),
     ds=pltpu.VMEM((2, 3 * T, T), BF),
+    hat=pltpu.VMEM((T, D), F32),
+    inv=pltpu.VMEM((T, 128), F32),
     p_own=pltpu.VMEM((16, 3 * T, T), F32),
     p_nb=pltpu.VMEM((2, 16, T, T), F32),
     delta=pltpu.VMEM((16, 1, T), F32),
@@ -419,7 +421,10 @@
         sends.append(copy)
 
     def norm(h, at):
-        hat, _ = moments(wide(s.x_v, h).astype(F32))
+        hat, inv = moments(wide(s.x_v, h).astype(F32))
+        if h == 1:
+            s.hat[...] = hat
+            s.inv[...] = jnp.broadcast_to(inv, (T, 128))
         s.n_v[pl.ds(at * T, T), :] = (hat * gain[...]).astype(BF)
 
     norm(1, 0)
@@ -477,10 +482,13 @@
             for n in (1, 3, 2):
                 outs.relay_y(outs.from_z(n))
 
-        res = nn(s.n_v[...], jnp.concatenate([s.w_v[g, n] for n in range(3)], axis=1))
+        own_res = nn(s.n_v[:T, :], jnp.concatenate([s.w_v[g, n] for n in range(3)], axis=1))
+        near_res = nn(s.n_v[T:, :], jnp.concatenate([s.w_v[g, 1], s.w_v[g, 2]], axis=1))
         for n in range(3):
-            s.qkv[n, g] = res[:, n * 128 : (n + 1) * 128].astype(BF)
-        vt = jnp.transpose(res[:, 256:]).astype(BF)
+            s.qkv[n, g, :T, :] = own_res[:, n * 128 : (n + 1) * 128].astype(BF)
+        for n in range(2):
+            s.qkv[n + 1, g, T:, :] = near_res[:, n * 128 : (n + 1) * 128].astype(BF)
+        vt = jnp.transpose(jnp.concatenate([own_res[:, 256:], near_res[:, 128:]], axis=0)).astype(BF)
         query = s.qkv[0, g, own_rows, :] * eighth
         scores = [nt(s.qkv[1, g], only(query, hh)) for hh in range(2)]
         parts = []
@@ -514,12 +522,14 @@
         outs.ready(outs.from_z(n))
     for i in range(1, G):
         remote(s.d_v.at[c], s.d_v.at[c], s.s_d.at[i], s.r_d.at[i], members[i]).wait_recv()
-    s.acc[...] = jnp.zeros_like(s.acc)
-
-    def out(g):
-        s.acc[...] += nn(s.mix[g], s.o_v[g]).astype(BF).astype(F32)
-
-    loop(G, out)
+    def out(m):
+        cols = pl.ds(pl.multiple_of(m * 256, 256), 256)
+        total = nn(s.mix[0], s.o_v[0, :, cols]).astype(BF).astype(F32)
+        for g in range(1, G):
+            total = total + nn(s.mix[g], s.o_v[g, :, cols]).astype(BF).astype(F32)
+        s.acc[:, cols] = total
+
+    loop(4, out)
     updated = (wide(s.x_v, 1).astype(F32) + s.acc[...]).astype(BF)
     dec_all = jnp.concatenate([s.d_v[g] for g in range(G)], axis=1)
     s.f_own[...] = nt(dec_all, updated).astype(BF)
@@ -569,6 +579,12 @@
                 sc = nt(s.qkv[1, g, own_rows, :], only(query, hh))
                 s.p_nb[side, n] = jnp.exp(sc - s.mlh[side, 0, n]) * s.mlh[side, 1, n]
 
+    def near_queries(m):
+        both = nn(s.n_v[T:, :], jnp.concatenate([s.w_v[2 * m, 0], s.w_v[2 * m + 1, 0]], axis=1)).astype(BF)
+        s.qkv[0, 2 * m, T:, :] = both[:, :128]
+        s.qkv[0, 2 * m + 1, T:, :] = both[:, 128:]
+
+    loop(2, near_queries)
     loop(4, near)
 
     fetch.wait()
@@ -598,6 +614,7 @@
     loop(L, observe)
     s.came[b] = s.am[b]
 
+    loop(2, lambda m: near_queries(m + 2))
     loop(4, lambda g: near(g + 4))
 
     index_t = jnp.transpose(index.astype(F32))[:VP].astype(jnp.int32)
@@ -721,7 +738,7 @@
         swaps[n]()
         loop(4, lambda g: other(g + 4 * n))
 
-    hat, inv = moments(wide(s.x_v, 1).astype(F32))
+    hat, inv = s.hat[...], s.inv[:, :1]
     grad_hat = s.acc[...] * gain[...]
     mean = jnp.sum(grad_hat, axis=-1, keepdims=True) * (1.0 / D)
     cross = jnp.sum(grad_hat * hat, axis=-1, keepdims=True) * (1.0 / D)

time: 120 us -> 119 us (level)
  no operation moved by 1% of the time
where the time goes in v6:
time: 119 us
  Pallas kernels  118 us (99%)
    pallas_call x1, Pallas kernels, call(): pl.pallas_call(kernel, out_shape=out_shape, in_specs=in_specs, out_specs=...  116 us

profile of v6, /device:TPU:1, one launch (start us, length us, event | category | flops | bytes accessed | tf_op | source)
XLA Modules:
  0.0 118.9 jit_solution(13799334553669005481)
XLA Ops:
  0.6 116.0 %whole.1 = (bf16[16,16,128]{2,1,0:T(8,128)(2,1)}, bf16[4,512,128]{2,1,0:T(8,128)(2,1)}) custom-call(bf16[4,512,128]{2,1,0:T(8,128)(2,1)} %state.3, bf16[1024,128]{1,0:T(8,128)(2,1)} %wq.1, bf16[1024,128]{1,0:T(8,128)(2,1)} %wk.1, bf16[1024,128]{1,0:T(8,128)(2,1)} %wv.1, bf16[128,1024]{1,0:T(8,128)(2,1)} %wo.1, bf16[69,128]{1,0:T(8,128)(2,1)} %bitcast.11, ...), custom_call_target="tpu_custom_call" | custom-call | tf_op jit(solution)/shard_map/whole/pallas_call | solution.py:89
  116.6 2.3 %finish.1 = (f32[16,16,128]{2,1,0:T(8,128)}, f32[4,512,128]{2,1,0:T(8,128)}) custom-call(bf16[16,16,128]{2,1,0:T(8,128)(2,1)} %get-tuple-element.6.low, bf16[4,512,128]{2,1,0:T(8,128)(2,1)} %get-tuple-element.7.back, bf16[4,512,128]{2,1,0:T(8,128)(2,1)} %state.3, bf16[4,512,128]{2,1,0:T(8,128)(2,1)} %background.1), custom_call_target="tpu_custom_call" | custom-call | tf_op jit(solution)/shard_map/finish/pallas_call | solution.py:810

commit v7 on v6

--- a/solution.py
+++ b/solution.py
@@ -538,7 +538,7 @@
         copy = remote(s.f_own, s.fields.at[j_own], s.s_f.at[i], s.r_f.at[j_own], members[i])
         copy.start() if act else copy.wait_send()
 
-    for i in range(1, G):
+    for i in (2, 6, 1, 3, 5, 7, 4):
         send_fields(i, True)
     pl.when(away)(lambda: send_fields(0, True))
 
@@ -750,7 +750,7 @@
         copy = remote(s.mix.at[dev[1]], back.at[r, pl.ds(w * T, T)], s.s_y.at[i], s.r_y.at[j_own], dev)
         copy.start() if act else copy.wait_send()
 
-    for i in range(1, G):
+    for i in (2, 6, 1, 3, 5, 7, 4):
         send_back(i, True)
     pl.when(away)(lambda: send_back(0, True))
 

time: 119 us -> 119 us (level)
  no operation moved by 1% of the time
where the time goes in v7:
time: 119 us
  Pallas kernels  118 us (99%)
    pallas_call x1, Pallas kernels, call(): pl.pallas_call(kernel, out_shape=out_shape, in_specs=in_specs, out_specs=...  116 us

profile of v7, /device:TPU:1, one launch (start us, length us, event | category | flops | bytes accessed | tf_op | source)
XLA Modules:
  0.0 118.6 jit_solution(8635475308297520545)
XLA Ops:
  0.6 115.7 %whole.1 = (bf16[16,16,128]{2,1,0:T(8,128)(2,1)}, bf16[4,512,128]{2,1,0:T(8,128)(2,1)}) custom-call(bf16[4,512,128]{2,1,0:T(8,128)(2,1)} %state.3, bf16[1024,128]{1,0:T(8,128)(2,1)} %wq.1, bf16[1024,128]{1,0:T(8,128)(2,1)} %wk.1, bf16[1024,128]{1,0:T(8,128)(2,1)} %wv.1, bf16[128,1024]{1,0:T(8,128)(2,1)} %wo.1, bf16[69,128]{1,0:T(8,128)(2,1)} %bitcast.11, ...), custom_call_target="tpu_custom_call" | custom-call | tf_op jit(solution)/shard_map/whole/pallas_call | solution.py:89
  116.3 2.3 %finish.1 = (f32[16,16,128]{2,1,0:T(8,128)}, f32[4,512,128]{2,1,0:T(8,128)}) custom-call(bf16[16,16,128]{2,1,0:T(8,128)(2,1)} %get-tuple-element.6.low, bf16[4,512,128]{2,1,0:T(8,128)(2,1)} %get-tuple-element.7.back, bf16[4,512,128]{2,1,0:T(8,128)(2,1)} %state.3, bf16[4,512,128]{2,1,0:T(8,128)(2,1)} %background.1), custom_call_target="tpu_custom_call" | custom-call | tf_op jit(solution)/shard_map/finish/pallas_call | solution.py:810
